TPU v7x, 32 devices: a whole 2x2x4 slice. The times are simulated.
32 devices in a mesh: groups: 2 (over x), ctx: 16 (over z, y, core).
Axes of the slice: x: 2, y: 2, z: 4, core: 2. Of those that a mesh axis runs over, the one named last changes fastest.
Arguments:
- queries: bfloat16 [16384, 2048], P(('groups', 'ctx')), parts along dimension 0, may hold values from -6 to 6
- keys: bfloat16 [256, 2048], P(('groups', 'ctx')), parts along dimension 0, may hold values from -6 to 6
- values: bfloat16 [256, 2048], P(('groups', 'ctx')), parts along dimension 0, may hold values from -6 to 6
- lengths: int32 [32], P(('groups', 'ctx')), parts along dimension 0, may hold values from 1 to 8, as said below
- dout: bfloat16 [16384, 2048], P(('groups', 'ctx')), parts along dimension 0, may hold values from -6 to 6
Outputs:
- attended: bfloat16 [16384, 2048], P(('groups', 'ctx')), parts along dimension 0
- query_grad: bfloat16 [16384, 2048], P(('groups', 'ctx')), parts along dimension 0
- key_grad: bfloat16 [256, 2048], P(('groups', 'ctx')), parts along dimension 0
- value_grad: bfloat16 [256, 2048], P(('groups', 'ctx')), parts along dimension 0
There are 2 independent parts, one for each index of `groups`. A program takes and returns all parts, laid end to end along the dimension named above; each array names one. Nothing has to cross between parts.
Inputs may be any that keep to these rules, and one draw needn't show every extreme that they name: `lengths`: every shard has at least one live position; shard 0 is full.
All inputs are finite; a program needn't handle non-finite values.
Results may differ from a plain program's by a relative error of at most 0.0014.
The roundings to bfloat16 on the way count: a program that leaves them out, or rounds other values in their place, can miss the bound.
Values may be sent and summed in bfloat16 or wider, within the bound.
No kernel may reach another device: no remote copies, remote signals or barrier semaphores. Data moves between devices by JAX's collectives and lax.ppermute only.
A program may use at most 128 MiB of HBM per device.

v0:
```python
import jax
import jax.numpy as jnp
from jax import lax
from jax.sharding import PartitionSpec as P

HEAD_DIM = 64


neg_fill = -1e30
head_block = 4


def split_heads(block):
    return block.reshape(block.shape[0], -1, head_block, HEAD_DIM).transpose(1, 0, 2, 3)


def join_heads(block):
    return block.transpose(1, 0, 2, 3).reshape(block.shape[1], -1)


def masked_scores(query_g, key_g, usable_g):
    logits = jnp.einsum(
        "tjd,mjd->jtm", query_g, key_g, preferred_element_type=jnp.float32
    ) * HEAD_DIM ** (-0.5)
    return jnp.where(usable_g[None, None, :] > 0, logits, neg_fill)


def memory_terms(grad_s, weights_low, query_g, grad_g):
    key_term = jnp.einsum(
        "jtm,tjd->mjd", grad_s, query_g, preferred_element_type=jnp.float32
    ) * HEAD_DIM ** (-0.5)
    value_term = jnp.einsum("jtm,tjd->mjd", weights_low, grad_g, preferred_element_type=jnp.float32)
    return (key_term, value_term)


def group_pass(pieces, usable):
    query_g, grad_g, key_g, value_g = pieces
    logits = masked_scores(query_g, key_g, usable)
    row_max = jnp.max(logits, axis=2)
    expo_w = jnp.exp(logits - row_max[..., None])
    row_sum = jnp.sum(expo_w, axis=2)
    softmax_w = expo_w / row_sum[..., None]
    weights_low = softmax_w.astype(jnp.bfloat16)
    attended = jnp.einsum(
        "jtm,mjd->tjd", weights_low, value_g, preferred_element_type=jnp.float32
    ).astype(jnp.bfloat16)
    delta = jnp.sum(grad_g.astype(jnp.float32) * attended.astype(jnp.float32), axis=2).T
    grad_p = jnp.einsum("tjd,mjd->jtm", grad_g, value_g, preferred_element_type=jnp.float32)
    grad_s = (softmax_w * (grad_p - delta[..., None])).astype(jnp.bfloat16)
    query_grad = (
        jnp.einsum("jtm,mjd->tjd", grad_s, key_g, preferred_element_type=jnp.float32)
        * HEAD_DIM ** (-0.5)
    ).astype(jnp.bfloat16)
    key_term, value_term = memory_terms(grad_s, weights_low, query_g, grad_g)
    return (attended, query_grad, key_term, value_term)


def per_device(queries, keys, values, lengths, dout):
    width = queries.shape[1]
    own_rows = keys.shape[0]
    own_usable = (jnp.arange(own_rows, dtype=jnp.int32) < lengths[0]).astype(jnp.bfloat16)
    every_key, every_value, every_usable = (
        lax.all_gather(keys, "ctx", axis=0, tiled=True),
        lax.all_gather(values, "ctx", axis=0, tiled=True),
        lax.all_gather(own_usable, "ctx", axis=0, tiled=True),
    )
    query_split = split_heads(queries)
    grad_split = split_heads(dout)
    results = lax.map(
        lambda pieces: group_pass(pieces, every_usable),
        (query_split, grad_split, split_heads(every_key), split_heads(every_value)),
    )
    terms = jnp.concatenate((join_heads(results[2]), join_heads(results[3])), axis=1)
    summed = lax.psum_scatter(terms, "ctx", scatter_dimension=0, tiled=True)
    attended = join_heads(results[0])
    query_grad = join_heads(results[1])
    key_grad = summed[:, :width].astype(jnp.bfloat16)
    value_grad = summed[:, width:].astype(jnp.bfloat16)
    return (attended, query_grad, key_grad, value_grad)


def solution(mesh):
    placed = (
        P(("groups", "ctx"), None),
        P(("groups", "ctx"), None),
        P(("groups", "ctx"), None),
        P(("groups", "ctx")),
        P(("groups", "ctx"), None),
    )
    return jax.shard_map(
        per_device,
        mesh=mesh,
        in_specs=placed,
        out_specs=(
            P(("groups", "ctx"), None),
            P(("groups", "ctx"), None),
            P(("groups", "ctx"), None),
            P(("groups", "ctx"), None),
        ),
        check_vma=False,
    )
```

profile of v0, /device:TPU:0, one launch (start us, length us, event | category | flops | bytes accessed | tf_op | source)
XLA Modules:
  0.0 257.6 jit_solution(6561422705755318541)
XLA Ops:
  10.2 35.0 %all-reduce = bf16[128]{0:T(256)(128)(2,1)S(1)} all-reduce(bf16[128]{0:T(256)(128)(2,1)S(1)} %dynamic-update-slice), channel_id=1, replica_groups=mesh['groups'=2,'ctx'=16] {'ctx'}, use_global_device_ids=true, to_apply=%add | all-reduce | flops 128 | bytes 512
  45.2 18.9 %all_gather.11 = bf16[128,2048]{1,0:T(8,128)(2,1)S(1)} all-gather(bf16[8,2048]{1,0:T(8,128)(2,1)} %param.8), channel_id=1, replica_groups=mesh['groups'=2,'ctx'=16] {'ctx'}, dimensions={0}, use_global_device_ids=true | all-gather | bytes 557056 | tf_op jit(solution)/shard_map/all_gather | solution.py:63
  64.5 21.2 %all_gather.9 = bf16[128,2048]{1,0:T(8,128)(2,1)S(1)} all-gather(bf16[8,2048]{1,0:T(8,128)(2,1)} %param.9), channel_id=1, replica_groups=mesh['groups'=2,'ctx'=16] {'ctx'}, dimensions={0}, use_global_device_ids=true | all-gather | bytes 557056 | tf_op jit(solution)/shard_map/all_gather | solution.py:64
  86.7 2.5 copy.41
  89.1 2.9 %copy.43 = bf16[512,2048]{0,1:T(8,128)(2,1)S(1)} copy(bf16[512,2048]{1,0:T(8,128)(2,1)} %param.11) | data formatting | bytes 4194304 | tf_op args[4]
  92.0 93.1 %while.16 = (s32[]{:T(128)}, bf16[8,512,4,64]{1,3,2,0:T(8,128)(2,1)}, bf16[8,512,4,64]{1,3,2,0:T(8,128)(2,1)}, f32[8,128,4,64]{1,3,2,0:T(8,128)}, f32[8,128,4,64...) while((s32[]{:T(128)}, ...), condition=%wide.region_4.5_spmd, body=%wide.region_0.4_spmd.sunk | while | flops 274106880 | bytes 7268345 | solution.py:69
  92.0 2.4 fusion.113
  94.5 2.3 fusion.117
  96.8 2.4 bitcast_dynamic-update-slice_fusion.2
  99.2 1.6 fusion.114
  100.9 1.9 fusion.116
  103.7 2.4 fusion.113
  106.1 2.3 fusion.117
  108.4 2.4 bitcast_dynamic-update-slice_fusion.2
  110.9 1.6 fusion.114
  112.5 1.9 fusion.116
  115.3 2.4 fusion.113
  117.8 2.3 fusion.117
  120.0 2.4 bitcast_dynamic-update-slice_fusion.2
  122.5 1.6 fusion.114
  124.1 1.9 fusion.116
  127.0 2.4 fusion.113
  129.4 2.3 fusion.117
  131.7 2.4 bitcast_dynamic-update-slice_fusion.2
  135.8 1.9 fusion.116
  138.6 2.4 fusion.113
  141.0 2.3 fusion.117
  143.3 2.4 bitcast_dynamic-update-slice_fusion.2
  145.8 1.6 fusion.114
  147.4 1.9 fusion.116
  150.2 2.4 fusion.113
  152.7 2.3 fusion.117
  155.0 2.4 bitcast_dynamic-update-slice_fusion.2
  159.0 1.9 fusion.116
  161.9 2.4 fusion.113
  164.3 2.3 fusion.117
  166.6 2.4 bitcast_dynamic-update-slice_fusion.2
  170.7 1.9 fusion.116
  173.5 2.4 fusion.113
  176.0 2.3 fusion.117
  178.2 2.4 bitcast_dynamic-update-slice_fusion.2
  180.7 1.6 fusion.114
  182.3 1.9 fusion.116
  185.2 1.7 pad_maximum_fusion
  186.8 1.8 copy.53
  188.7 4.1 %copy.44 = bf16[512,2048]{1,0:T(8,128)(2,1)} copy(bf16[512,2048]{0,1:T(8,128)(2,1)} %bitcast.155) | data formatting | bytes 4194304
  192.8 2.4 copy.45
  195.1 52.6 %reduce-scatter.4.cloned.1.call-done = f32[8,4096]{1,0:T(8,128)} async-done(((f32[128,4096]{1,0:T(8,128)}), f32[8,4096]{1,0:T(8,128)}) %reduce-scatter.4.cloned.1.call-update) | async-done | bytes 131088
  (47 shorter events, 19.0 us)
Async XLA Ops:
  7.2 79.5 %copy-start = (bf16[512,2048]{1,0:T(8,128)(2,1)S(1)}, bf16[512,2048]{1,0:T(8,128)(2,1)}, u32[]{:S(2)}) copy-start(bf16[512,2048]{1,0:T(8,128)(2,1)} %param.7) | copy-start | bytes 6291460
  7.2 240.5 %reduce-scatter.4.cloned.1.call-start = ((), (), s32[]{:S(2)}) async-start(), calls=%async_computation.1 | async-start | bytes 2228224
  188.7 4.1 %copy-start.1 = (bf16[8,512,4,64]{1,3,2,0:T(8,128)(2,1)S(1)}, bf16[8,512,4,64]{1,3,2,0:T(8,128)(2,1)}, u32[]{:S(2)}) copy-start(bf16[8,512,4,64]{1,3,2,0:T(8,128)(2,1)} %get-tuple-element.60) | copy-start | bytes 6291460
Sparse Core Ops, SparseCore 0:
  188.8 58.8 reduce-scatter.3
where the time goes:
time: 259 us; the launch traced here: 258 us
  matrix products  92.2 us (36%)
  blocking collectives  75.2 us (29%)
  waiting for transfers between devices  52.6 us (20%)
  local copies, waits for them, and re-layouts  19.4 us (7%)
  between operations  15.6 us (6%)
    unnamed x2, waiting for transfers between devices  52.6 us
    unnamed x1, blocking collectives  35 us
    all_gather x1, blocking collectives, per_device(): lax.all_gather(values, 'ctx', axis=0, tiled=True)  21.2 us
    sub x8, matrix products, group_pass(): expo_w = jnp.exp(logits - row_max[..., None])  19.5 us
    all_gather x1, blocking collectives, per_device(): lax.all_gather(keys, 'ctx', axis=0, tiled=True)  18.9 us
    dot_general x8, matrix products, group_pass(): jnp.einsum('jtm,mjd->tjd', weights_low, value_g, preferred_element_type=j...  18.9 us
    dot_general x8, matrix products, memory_terms(): jnp.einsum('jtm,tjd->mjd', weights_low, grad_g, preferred_element_type=jn...  18.2 us
    unnamed x15, local copies, waits for them, and re-layouts  18.1 us
  transfers between devices with their start and end apart: 1, of which 1 were waited for; matrix products, arithmetic and copies ran while one was open for 2% of the time, Pallas kernels for 0%

commit v1 on v0

v1 whole, which is shorter than its diff:
```python
import jax
import jax.numpy as jnp
from jax import lax
from jax.experimental import pallas as pl
from jax.experimental.pallas import tpu as pltpu
from jax.sharding import PartitionSpec as P

HEAD_DIM = 64
LANES = 128
SCALE = HEAD_DIM ** -0.5
NEG = -1e30
F32 = jnp.float32
BF16 = jnp.bfloat16

CHUNKS = (1.0,)
PAIRS_PER_STEP = 4


def dot(a, b, ca, cb):
    return lax.dot_general(a, b, (((ca,), (cb,)), ((), ())), preferred_element_type=F32)


def pair_pass(q, do, k2, v2, bias, tokens, memory):
    s = dot(k2, q, 1, 1).reshape(2, memory, tokens) + bias
    e = jnp.exp(s - jnp.max(s, axis=1, keepdims=True))
    p = e * (1.0 / jnp.sum(e, axis=1, keepdims=True))
    p_low = p.astype(BF16).reshape(2 * memory, tokens)
    att = dot(v2, p_low, 0, 0).astype(BF16)
    grad_p = dot(v2, do, 1, 1).reshape(2, memory, tokens)
    delta = (do.T.astype(F32) * att.astype(F32)).reshape(2, HEAD_DIM, tokens)
    delta = jnp.sum(delta, axis=1, keepdims=True)
    grad_s = (p * (grad_p - delta)).astype(BF16).reshape(2 * memory, tokens)
    dq = dot(k2, grad_s, 0, 0).astype(BF16)
    return att.T, dq.T, dot(grad_s, q, 1, 0), dot(p_low, do, 1, 0)


def attention(queries, dout, first, second, carried, offset, pairs):
    tokens, width = queries.shape
    half = first.shape[0]
    memory = 2 * half
    step = max(d for d in range(1, PAIRS_PER_STEP + 1) if pairs % d == 0 and offset % d == 0)
    grid = pairs // step
    block = step * LANES

    def body(*refs):
        q_ref, do_ref, ka_ref, kb_ref, va_ref, vb_ref, fa_ref, fb_ref = refs[:8]
        att_ref, dq_ref, lo_ref, hi_ref = refs[-4:]
        live = jnp.concatenate([fa_ref[...], fb_ref[...]], axis=0).astype(F32)
        bias = jnp.where(live[:, :1] > 0, 0.0, NEG)
        left = lax.broadcasted_iota(jnp.int32, (memory, LANES), 1) < HEAD_DIM
        zero = jnp.zeros((memory, LANES), BF16)

        def both(x):
            return jnp.concatenate([jnp.where(left, x, zero), jnp.where(left, zero, x)], axis=0)

        for i in range(step):
            c = pl.ds(i * LANES, LANES)
            k = jnp.concatenate([ka_ref[:, c], kb_ref[:, c]], axis=0) * jnp.asarray(SCALE, BF16)
            v = jnp.concatenate([va_ref[:, c], vb_ref[:, c]], axis=0)
            att, dq, dk, dv = pair_pass(q_ref[:, c], do_ref[:, c], both(k), both(v), bias, tokens, memory)
            att_ref[:, c] = att
            dq_ref[:, c] = dq
            dk = jnp.where(left, dk[:memory], dk[memory:]) * SCALE
            dv = jnp.where(left, dv[:memory], dv[memory:])
            for j, x in enumerate((dk, dv)):
                c2 = pl.ds((2 * i + j) * LANES, LANES)
                lo_ref[:, c2] = x[:half]
                hi_ref[:, c2] = x[half:]

    base = offset // step
    token_spec = pl.BlockSpec((tokens, block), lambda g: (0, g + base))
    k_spec = pl.BlockSpec((half, block), lambda g: (0, g))
    v_spec = pl.BlockSpec((half, block), lambda g: (0, g + grid))
    flag_spec = pl.BlockSpec((half, LANES), lambda g: (0, 2 * pairs))
    term_spec = pl.BlockSpec((half, 2 * block), lambda g: (0, g))
    extra = () if carried is None else tuple(carried)
    return pl.pallas_call(
        body,
        grid=(grid,),
        in_specs=[token_spec, token_spec, k_spec, k_spec, v_spec, v_spec, flag_spec, flag_spec]
        + [pl.BlockSpec(memory_space=pl.ANY)] * len(extra),
        out_specs=[token_spec, token_spec, term_spec, term_spec],
        out_shape=[jax.ShapeDtypeStruct((tokens, width), BF16)] * 2
        + [jax.ShapeDtypeStruct((half, 2 * pairs * LANES), F32)] * 2,
        input_output_aliases={8 + i: i for i in range(len(extra))},
        compiler_params=pltpu.CompilerParams(
            dimension_semantics=("arbitrary",), vmem_limit_bytes=48 * 2**20
        ),
    )(queries, dout, first, second, first, second, first, second, *extra)


def split_pairs(total):
    ends, done = [0], 0.0
    for share in CHUNKS:
        done += share
        ends.append(min(total, round(done * total)))
    ends[-1] = total
    return [(a, b - a) for a, b in zip(ends, ends[1:]) if b > a]


def solution(mesh):
    n = mesh.shape["ctx"]
    bits = [1 << b for b in range(n.bit_length() - 1)]
    assert n == 1 << len(bits)

    def swap(x, bit):
        return lax.ppermute(x, "ctx", [(i, i ^ bit) for i in range(n)])

    def gather(x):
        for bit in bits[:0:-1]:
            x = jnp.concatenate([x, swap(x, bit)], axis=0)
        return x, swap(x, bits[0])

    def scatter(lo, hi):
        x = lo + swap(hi, bits[0])
        for bit in bits[1:]:
            half = x.shape[0] // 2
            x = x[:half] + swap(x[half:], bit)
        return x

    def per_device(queries, keys, values, lengths, dout):
        rows, width = keys.shape
        live = lax.broadcasted_iota(jnp.int32, (rows, LANES), 0) < lengths[0]
        chunks = split_pairs(width // LANES)
        gathered = []
        for start, pairs in chunks:
            cols = slice(start * LANES, (start + pairs) * LANES)
            packed = jnp.concatenate([keys[:, cols], values[:, cols], live.astype(BF16)], axis=1)
            gathered.append(gather(packed))
        carried, sums = None, []
        for (start, pairs), (first, second) in zip(chunks, gathered):
            *carried, lo, hi = attention(queries, dout, first, second, carried, start, pairs)
            sums.append(scatter(lo, hi))
        total = jnp.concatenate(sums, axis=1).reshape(rows, width // LANES, 2, LANES)
        key_grad = total[:, :, 0].reshape(rows, width).astype(BF16)
        value_grad = total[:, :, 1].reshape(rows, width).astype(BF16)
        return (*carried, key_grad, value_grad)

    spec = P(("groups", "ctx"), None)
    return jax.shard_map(
        per_device,
        mesh=mesh,
        in_specs=(spec, spec, spec, P(("groups", "ctx")), spec),
        out_specs=(spec,) * 4,
        check_vma=False,
    )
```

time: 259 us -> 76.7 us (0.30)
  matrix products: 92.2 us -> 0 us
  blocking collectives: 75.2 us -> 0 us
  local copies, waits for them, and re-layouts: 19.4 us -> 2.36 us
  Pallas kernels: 0 us -> 15.2 us
  between operations: 15.6 us -> 1.34 us
  starting transfers between devices: 0.04 us -> 13 us
  waiting for transfers between devices: 52.6 us -> 41 us
    dot_general x40 -> x0, matrix products: 72.7 us -> none  [the longest x8 18.9 us: group_pass(): jnp.einsum('jtm,mjd->tjd', weights_low, value_g, preferred_element_type=j...]
    unnamed x2 -> x0, waiting for transfers between devices: 52.6 us -> none
    ppermute x0 -> x8, waiting for transfers between devices: none -> 41 us  [swap(): return lax.ppermute(x, 'ctx', [(i, i ^ bit) for i in range(n)])]
    all_gather x2 -> x0, blocking collectives: 40.1 us -> none  [the longest x1 21.2 us: per_device(): lax.all_gather(values, 'ctx', axis=0, tiled=True)]
    unnamed x1 -> x0, blocking collectives: 35 us -> none
    sub x8 -> x0, matrix products: 19.5 us -> none  [group_pass(): expo_w = jnp.exp(logits - row_max[..., None])]
    unnamed x15 -> x2, local copies, waits for them, and re-layouts: 18.1 us -> 1.59 us
    pallas_call x0 -> x1, Pallas kernels: none -> 15.2 us  [attention(): pl.pallas_call(body, grid=(grid,), in_specs=[token_spec, token_spec, k_sp...]
  transfers between devices with their start and end apart: 1 -> 8, of which waited for: 1 -> 8; matrix products, arithmetic and copies ran while one was open for 2% -> 0% of each run, Pallas kernels for 0% -> 0%
where the time goes in v1:
time: 76.7 us; the launch traced here: 76.3 us
  waiting for transfers between devices  41 us (53%)
  Pallas kernels  15.2 us (20%)
  starting transfers between devices  13 us (17%)
  other arithmetic  3.43 us (4%)
  local copies, waits for them, and re-layouts  2.36 us (3%)
  between operations  1.34 us (2%)
    ppermute x8, waiting for transfers between devices, swap(): return lax.ppermute(x, 'ctx', [(i, i ^ bit) for i in range(n)])  41 us
    pallas_call x1, Pallas kernels, attention(): pl.pallas_call(body, grid=(grid,), in_specs=[token_spec, token_spec, k_sp...  15.2 us
    ppermute x8, starting transfers between devices, swap(): return lax.ppermute(x, 'ctx', [(i, i ^ bit) for i in range(n)])  13 us
    concatenate x3, other arithmetic, gather(): x = jnp.concatenate([x, swap(x, bit)], axis=0)  2.41 us
    unnamed x2, local copies, waits for them, and re-layouts  1.59 us
  transfers between devices with their start and end apart: 8, of which 8 were waited for; matrix products, arithmetic and copies ran while one was open for 0% of the time, Pallas kernels for 0%

profile of v1, /device:TPU:0, one launch (start us, length us, event | category | flops | bytes accessed | tf_op | source)
XLA Modules:
  0.0 76.3 jit_solution(12867181981796567102)
XLA Ops:
  1.3 0.1 iota.7
  1.4 0.8 %pad_maximum_fusion.3 = bf16[8,4224]{1,0:T(8,128)(2,1)S(1)} fusion(bf16[8,128]{1,0:T(8,128)(2,1)S(1)} %iota.7, bf16[8,2048]{1,0:T(8,128)(2,1)} %param.7, bf16[8,2048]{1,0:T(8,128)(2,1)} %param.6), kind=kLoop, calls=%fused_computation.7 | loop fusion | flops 202752 | bytes 135168 | tf_op jit(solution)/shard_map/concatenate | solution.py:128
  2.1 4.0 %collective-permute-start = (bf16[8,4224]{1,0:T(8,128)(2,1)S(1)}, bf16[8,4224]{1,0:T(8,128)(2,1)S(1)}, u32[]{:S(2)}, u32[]{:S(2)}) collective-permute-start(bf16[8,4224]{1,0:T(8,128)(2,1)S(1)} %pad_maximum_fusion.3), channel_id=1, source_target_pairs={{0,8},{1,9},{2,10},{3,11},{4,12},{5,13},{6,14},{7,15},{8,0},{9,1},... | collective-permute-start | bytes 202760 | tf_op jit(solution)/shard_map/ppermute | solution.py:107
  6.2 3.7 %collective-permute-done = bf16[8,4224]{1,0:T(8,128)(2,1)S(1)} collective-permute-done((bf16[8,4224]{1,0:T(8,128)(2,1)S(1)}, bf16[8,4224]{1,0:T(8,128)(2,1)S(1)}, u32[]{:S(2)}, u32[]{:S(2)}) %collective-permute-start) | collective-permute-done | bytes 67616 | tf_op jit(solution)/shard_map/ppermute | solution.py:107
  9.9 0.8 %pad_maximum_fusion.2 = bf16[16,4224]{1,0:T(8,128)(2,1)S(1)} fusion(bf16[8,4224]{1,0:T(8,128)(2,1)S(1)} %collective-permute-done, bf16[8,128]{1,0:T(8,128)(2,1)S(1)} %iota.7, bf16[8,2048]{1,0:T(8,128)(2,1)} %param.7, bf16[8,2048]{1,0:T(8,128)(2,1)} %param.6), kind=kLoop, calls=%fused_computation.4 | loop fusion | flops 540672 | bytes 270336 | tf_op jit(solution)/shard_map/concatenate | solution.py:111
  10.7 0.7 collective-permute-start.1
  11.3 4.4 %collective-permute-done.1 = bf16[16,4224]{1,0:T(8,128)(2,1)S(1)} collective-permute-done((bf16[16,4224]{1,0:T(8,128)(2,1)S(1)}, bf16[16,4224]{1,0:T(8,128)(2,1)S(1)}, u32[]{:S(2)}, u32[]{:S(2)}) %collective-permute-start.1) | collective-permute-done | bytes 135200 | tf_op jit(solution)/shard_map/ppermute | solution.py:107
  15.8 0.8 %pad_maximum_fusion.1 = bf16[32,4224]{1,0:T(8,128)(2,1)S(1)} fusion(bf16[16,4224]{1,0:T(8,128)(2,1)S(1)} %collective-permute-done.1, bf16[8,4224]{1,0:T(8,128)(2,1)S(1)} %collective-permute-done, bf16[8,128]{1,0:T(8,128)(2,1)S(1)} %iota.7, bf16[8,2048]{1,0:T(8,128)(2,1)} %param.7, bf16[8,2048]{1,0:T(8,128)(2,1)} %param.6), kind=kLoop, calls=%fused_computation.2 | loop fusion | flops 1351680 | bytes 540672 | tf_op jit(solution)/shard_map/concatenate | solution.py:111
  16.6 1.8 %collective-permute-start.2 = (bf16[32,4224]{1,0:T(8,128)(2,1)S(1)}, bf16[32,4224]{1,0:T(8,128)(2,1)S(1)}, u32[]{:S(2)}, u32[]{:S(2)}) collective-permute-start(bf16[32,4224]{1,0:T(8,128)(2,1)S(1)} %pad_maximum_fusion.1), channel_id=1, source_target_pairs={{0,2},{1,3},{2,0},{3,1},{4,6},{5,7},{6,4},{7,5},{8,10},{9,11},{10,... | collective-permute-start | bytes 811016 | tf_op jit(solution)/shard_map/ppermute | solution.py:107
  18.4 4.7 %collective-permute-done.2 = bf16[32,4224]{1,0:T(8,128)(2,1)S(1)} collective-permute-done((bf16[32,4224]{1,0:T(8,128)(2,1)S(1)}, bf16[32,4224]{1,0:T(8,128)(2,1)S(1)}, u32[]{:S(2)}, u32[]{:S(2)}) %collective-permute-start.2) | collective-permute-done | bytes 270368 | tf_op jit(solution)/shard_map/ppermute | solution.py:107
  23.1 0.8 %pad_maximum_fusion.refs_2_.refs_4_.refs_6_ = bf16[64,4224]{1,0:T(8,128)(2,1)S(1)} fusion(bf16[32,4224]{1,0:T(8,128)(2,1)S(1)} %collective-permute-done.2, bf16[16,4224]{1,0:T(8,128)(2,1)S(1)} %collective-permute-done.1, bf16[8,4224]{1,0:T(8,128)(2,1)S(1)} %collective-permute-done, bf16[8,128]{1,0:T(8,128)(2,1)S(1)} %iota.7, bf16[8,2048]{1,0:T(8,128)(2,1)} %param.7, ...), kind=kLoop, calls=%fused_computation | loop fusion | flops 3244032 | bytes 1081344 | tf_op jit(solution)/shard_map/concatenate | solution.py:111
  23.9 0.1 collective-permute-start.3
  24.0 1.9 %collective-permute-done.3.refs_3_.refs_5_.refs_7_ = bf16[64,4224]{1,0:T(8,128)(2,1)S(1)} collective-permute-done((bf16[64,4224]{1,0:T(8,128)(2,1)S(1)}, bf16[64,4224]{1,0:T(8,128)(2,1)S(1)}, u32[]{:S(2)}, u32[]{:S(2)}) %collective-permute-start.3) | collective-permute-done | bytes 540704 | tf_op jit(solution)/shard_map/ppermute | solution.py:107
  25.9 0.0 copy-start
  25.9 1.6 %copy-done = bf16[512,2048]{1,0:T(8,128)(2,1)S(1)} copy-done((bf16[512,2048]{1,0:T(8,128)(2,1)S(1)}, bf16[512,2048]{1,0:T(8,128)(2,1)}, u32[]{:S(2)}) %copy-start) | copy-done | bytes 2097176
  27.5 15.2 %shard_map.84 = (bf16[512,2048]{1,0:T(8,128)(2,1)}, bf16[512,2048]{1,0:T(8,128)(2,1)}, f32[64,4096]{1,0:T(8,128)S(1)}, f32[64,4096]{1,0:T(8,128)S(1)}) custom-call(bf16[512,2048]{1,0:T(8,128)(2,1)S(1)} %copy-done, bf16[512,2048]{1,0:T(8,128)(2,1)} %refs_1_.1, bf16[64,4224]{1,0:T(8,128)(2,1)S(1)} %pad_maximum_fusion.refs_2_.refs_4_.refs_6_, ...), custom_call_target="tpu_custom_call" | custom-call | tf_op jit(solution)/shard_map/pallas_call | solution.py:77
  42.7 0.1 collective-permute-start.4
  42.8 2.5 %collective-permute-done.4 = f32[64,4096]{1,0:T(8,128)S(1)} collective-permute-done((f32[64,4096]{1,0:T(8,128)S(1)}, f32[64,4096]{1,0:T(8,128)S(1)}, u32[]{:S(2)}, u32[]{:S(2)}) %collective-permute-start.4) | collective-permute-done | bytes 1048608 | tf_op jit(solution)/shard_map/ppermute | solution.py:107
  45.3 0.1 add.12
  45.5 1.8 %collective-permute-start.5 = (f32[32,4096]{1,0:T(8,128)S(1)}, f32[32,4096]{1,0:T(8,128)S(1)}, u32[]{:S(2)}, u32[]{:S(2)}) collective-permute-start(f32[32,4096]{1,0:T(8,128)S(1)} %slice.35), channel_id=1, source_target_pairs={{0,2},{1,3},{2,0},{3,1},{4,6},{5,7},{6,4},{7,5},{8,10},{9,11},{10,... | collective-permute-start | bytes 1572872 | tf_op jit(solution)/shard_map/ppermute | solution.py:107
  47.3 12.2 %collective-permute-done.5 = f32[32,4096]{1,0:T(8,128)S(1)} collective-permute-done((f32[32,4096]{1,0:T(8,128)S(1)}, f32[32,4096]{1,0:T(8,128)S(1)}, u32[]{:S(2)}, u32[]{:S(2)}) %collective-permute-start.5) | collective-permute-done | bytes 524320 | tf_op jit(solution)/shard_map/ppermute | solution.py:107
  59.5 0.1 slice_add_fusion
  59.6 1.0 %collective-permute-start.6 = (f32[16,4096]{1,0:T(8,128)S(1)}, f32[16,4096]{1,0:T(8,128)S(1)}, u32[]{:S(2)}, u32[]{:S(2)}) collective-permute-start(f32[16,4096]{1,0:T(8,128)S(1)} %slice.37), channel_id=1, source_target_pairs={{0,4},{1,5},{2,6},{3,7},{4,0},{5,1},{6,2},{7,3},{8,12},{9,13},{10,... | collective-permute-start | bytes 786440 | tf_op jit(solution)/shard_map/ppermute | solution.py:107
  60.6 6.6 %collective-permute-done.6 = f32[16,4096]{1,0:T(8,128)S(1)} collective-permute-done((f32[16,4096]{1,0:T(8,128)S(1)}, f32[16,4096]{1,0:T(8,128)S(1)}, u32[]{:S(2)}, u32[]{:S(2)}) %collective-permute-start.6) | collective-permute-done | bytes 262176 | tf_op jit(solution)/shard_map/ppermute | solution.py:107
  67.3 3.5 %collective-permute-start.7 = (f32[8,4096]{1,0:T(8,128)S(1)}, f32[8,4096]{1,0:T(8,128)S(1)}, u32[]{:S(2)}, u32[]{:S(2)}) collective-permute-start(f32[8,4096]{1,0:T(8,128)S(1)} %slice.39), channel_id=1, source_target_pairs={{0,8},{1,9},{2,10},{3,11},{4,12},{5,13},{6,14},{7,15},{8,0},{9,1},... | collective-permute-start | bytes 393224 | tf_op jit(solution)/shard_map/ppermute | solution.py:107
  70.8 4.9 %collective-permute-done.7 = f32[8,4096]{1,0:T(8,128)S(1)} collective-permute-done((f32[8,4096]{1,0:T(8,128)S(1)}, f32[8,4096]{1,0:T(8,128)S(1)}, u32[]{:S(2)}, u32[]{:S(2)}) %collective-permute-start.7) | collective-permute-done | bytes 131104 | tf_op jit(solution)/shard_map/ppermute | solution.py:107
  75.6 0.6 slice_bitcast_fusion
  (6 shorter events, 0.1 us)
Async XLA Ops:
  2.1 7.7 %collective-permute-start = (bf16[8,4224]{1,0:T(8,128)(2,1)S(1)}, bf16[8,4224]{1,0:T(8,128)(2,1)S(1)}, u32[]{:S(2)}, u32[]{:S(2)}) collective-permute-start(bf16[8,4224]{1,0:T(8,128)(2,1)S(1)} %pad_maximum_fusion.3), channel_id=1, source_target_pairs={{0,8},{1,9},{2,10},{3,11},{4,12},{5,13},{6,14},{7,15},{8,0},{9,1},... | collective-permute-start | bytes 202760 | tf_op jit(solution)/shard_map/ppermute | solution.py:107
  10.7 5.1 %collective-permute-start.1 = (bf16[16,4224]{1,0:T(8,128)(2,1)S(1)}, bf16[16,4224]{1,0:T(8,128)(2,1)S(1)}, u32[]{:S(2)}, u32[]{:S(2)}) collective-permute-start(bf16[16,4224]{1,0:T(8,128)(2,1)S(1)} %pad_maximum_fusion.2), channel_id=1, source_target_pairs={{0,4},{1,5},{2,6},{3,7},{4,0},{5,1},{6,2},{7,3},{8,12},{9,13},{10,... | collective-permute-start | bytes 405512 | tf_op jit(solution)/shard_map/ppermute | solution.py:107
  16.6 6.5 %collective-permute-start.2 = (bf16[32,4224]{1,0:T(8,128)(2,1)S(1)}, bf16[32,4224]{1,0:T(8,128)(2,1)S(1)}, u32[]{:S(2)}, u32[]{:S(2)}) collective-permute-start(bf16[32,4224]{1,0:T(8,128)(2,1)S(1)} %pad_maximum_fusion.1), channel_id=1, source_target_pairs={{0,2},{1,3},{2,0},{3,1},{4,6},{5,7},{6,4},{7,5},{8,10},{9,11},{10,... | collective-permute-start | bytes 811016 | tf_op jit(solution)/shard_map/ppermute | solution.py:107
  23.9 2.0 %collective-permute-start.3 = (bf16[64,4224]{1,0:T(8,128)(2,1)S(1)}, bf16[64,4224]{1,0:T(8,128)(2,1)S(1)}, u32[]{:S(2)}, u32[]{:S(2)}) collective-permute-start(bf16[64,4224]{1,0:T(8,128)(2,1)S(1)} %pad_maximum_fusion.refs_2_.refs_4_.refs_6_), channel_id=1, source_target_pairs={{0,1},{1,0},{2,3},{3,2},{4,5},{5,4},{6,7},{7,6},{8,9},{9,8},{10,11... | collective-permute-start | bytes 1622024 | tf_op jit(solution)/shard_map/ppermute | solution.py:107
  25.9 1.6 %copy-start = (bf16[512,2048]{1,0:T(8,128)(2,1)S(1)}, bf16[512,2048]{1,0:T(8,128)(2,1)}, u32[]{:S(2)}) copy-start(bf16[512,2048]{1,0:T(8,128)(2,1)} %refs_0_.1) | copy-start | bytes 6291460
  42.7 2.7 %collective-permute-start.4 = (f32[64,4096]{1,0:T(8,128)S(1)}, f32[64,4096]{1,0:T(8,128)S(1)}, u32[]{:S(2)}, u32[]{:S(2)}) collective-permute-start(f32[64,4096]{1,0:T(8,128)S(1)} %get-tuple-element.11), channel_id=1, source_target_pairs={{0,1},{1,0},{2,3},{3,2},{4,5},{5,4},{6,7},{7,6},{8,9},{9,8},{10,11... | collective-permute-start | bytes 3145736 | tf_op jit(solution)/shard_map/ppermute | solution.py:107
  45.5 14.0 %collective-permute-start.5 = (f32[32,4096]{1,0:T(8,128)S(1)}, f32[32,4096]{1,0:T(8,128)S(1)}, u32[]{:S(2)}, u32[]{:S(2)}) collective-permute-start(f32[32,4096]{1,0:T(8,128)S(1)} %slice.35), channel_id=1, source_target_pairs={{0,2},{1,3},{2,0},{3,1},{4,6},{5,7},{6,4},{7,5},{8,10},{9,11},{10,... | collective-permute-start | bytes 1572872 | tf_op jit(solution)/shard_map/ppermute | solution.py:107
  59.6 7.6 %collective-permute-start.6 = (f32[16,4096]{1,0:T(8,128)S(1)}, f32[16,4096]{1,0:T(8,128)S(1)}, u32[]{:S(2)}, u32[]{:S(2)}) collective-permute-start(f32[16,4096]{1,0:T(8,128)S(1)} %slice.37), channel_id=1, source_target_pairs={{0,4},{1,5},{2,6},{3,7},{4,0},{5,1},{6,2},{7,3},{8,12},{9,13},{10,... | collective-permute-start | bytes 786440 | tf_op jit(solution)/shard_map/ppermute | solution.py:107
  67.3 8.4 %collective-permute-start.7 = (f32[8,4096]{1,0:T(8,128)S(1)}, f32[8,4096]{1,0:T(8,128)S(1)}, u32[]{:S(2)}, u32[]{:S(2)}) collective-permute-start(f32[8,4096]{1,0:T(8,128)S(1)} %slice.39), channel_id=1, source_target_pairs={{0,8},{1,9},{2,10},{3,11},{4,12},{5,13},{6,14},{7,15},{8,0},{9,1},... | collective-permute-start | bytes 393224 | tf_op jit(solution)/shard_map/ppermute | solution.py:107

commit v2 on v1

v2 whole, which is shorter than its diff:
```python
import jax
import jax.numpy as jnp
from jax import lax
from jax.experimental import pallas as pl
from jax.experimental.pallas import tpu as pltpu
from jax.sharding import PartitionSpec as P

HEAD_DIM = 64
LANES = 128
SCALE = HEAD_DIM ** -0.5
NEG = -1e30
F32 = jnp.float32
BF16 = jnp.bfloat16

CHUNKS = (((8 / 16,), 0), ((8 / 16,), 1))
PAIRS_PER_STEP = 4
COST = 1
TIE = False


def dot(a, b, ca, cb):
    return lax.dot_general(a, b, (((ca,), (cb,)), ((), ())), preferred_element_type=F32)


def pair_pass(q, do, k2, v2, bias, tokens, memory):
    s = dot(k2, q, 1, 1).reshape(2, memory, tokens) + bias
    e = jnp.exp(s - jnp.max(s, axis=1, keepdims=True))
    p = e * (1.0 / jnp.sum(e, axis=1, keepdims=True))
    p_low = p.astype(BF16).reshape(2 * memory, tokens)
    att = dot(v2, p_low, 0, 0).astype(BF16)
    grad_p = dot(v2, do, 1, 1).reshape(2, memory, tokens)
    delta = (do.T.astype(F32) * att.astype(F32)).reshape(2, HEAD_DIM, tokens)
    delta = jnp.sum(delta, axis=1, keepdims=True)
    grad_s = (p * (grad_p - delta)).astype(BF16).reshape(2 * memory, tokens)
    dq = dot(k2, grad_s, 0, 0).astype(BF16)
    return att.T, dq.T, dot(grad_s, q, 1, 0), dot(p_low, do, 1, 0)


def attention(queries, dout, first, second, results, terms, offset, place, pairs, total):
    tokens, width = queries.shape
    half = first.shape[0]
    memory = 2 * half
    most = max(1, PAIRS_PER_STEP * 128 // memory)
    step = max(d for d in range(1, most + 1) if all(x % d == 0 for x in (pairs, offset, place, total)))
    block = step * LANES

    def body(*refs):
        q_ref, do_ref, ka_ref, kb_ref, va_ref, vb_ref, fa_ref, fb_ref = refs[:8]
        att_ref, dq_ref, lo_ref, hi_ref = refs[-4:]
        live = jnp.concatenate([fa_ref[...], fb_ref[...]], axis=0).astype(F32)
        bias = jnp.where(live[:, :1] > 0, 0.0, NEG)
        left = lax.broadcasted_iota(jnp.int32, (memory, LANES), 1) < HEAD_DIM
        zero = jnp.zeros((memory, LANES), BF16)

        def both(x):
            return jnp.concatenate([jnp.where(left, x, zero), jnp.where(left, zero, x)], axis=0)

        for i in range(step):
            c = pl.ds(i * LANES, LANES)
            k = jnp.concatenate([ka_ref[:, c], kb_ref[:, c]], axis=0) * jnp.asarray(SCALE, BF16)
            v = jnp.concatenate([va_ref[:, c], vb_ref[:, c]], axis=0)
            att, dq, dk, dv = pair_pass(q_ref[:, c], do_ref[:, c], both(k), both(v), bias, tokens, memory)
            att_ref[:, c] = att
            dq_ref[:, c] = dq
            dk = jnp.where(left, dk[:memory], dk[memory:]) * SCALE
            dv = jnp.where(left, dv[:memory], dv[memory:])
            tc = pl.ds(2 * i * LANES, 2 * LANES)
            lo_ref[:, tc] = jnp.concatenate([dk[:half], dv[:half]], axis=1)
            hi_ref[:, tc] = jnp.concatenate([dk[half:], dv[half:]], axis=1)

    def cols(rows, width, start):
        return pl.BlockSpec((rows, width), lambda g: (0, g + start))

    token_spec = cols(tokens, block, offset // step)
    k_spec = cols(half, block, place // step)
    v_spec = cols(half, block, (total + place) // step)
    flag_spec = pl.BlockSpec((half, LANES), lambda g: (0, 2 * total))
    term_spec = cols(half, 2 * block, place // step)
    extra = {}
    if results is not None:
        extra.update(enumerate(results))
    if terms is not None:
        extra.update(enumerate(terms, 2))
    scratch = min(52, 12 + step * memory * tokens * 2 * 4 * 4 // 2**20)
    return pl.pallas_call(
        body,
        grid=(pairs // step,),
        in_specs=[token_spec, token_spec, k_spec, k_spec, v_spec, v_spec, flag_spec, flag_spec]
        + [pl.BlockSpec(memory_space=pl.ANY)] * len(extra),
        out_specs=[token_spec, token_spec, term_spec, term_spec],
        out_shape=[jax.ShapeDtypeStruct((tokens, width), BF16)] * 2
        + [jax.ShapeDtypeStruct((half, 2 * total * LANES), F32)] * 2,
        input_output_aliases={8 + i: out for i, out in enumerate(extra)},
        compiler_params=pltpu.CompilerParams(
            dimension_semantics=("arbitrary",), vmem_limit_bytes=scratch * 2**20
        ),
        cost_estimate=pl.CostEstimate(
            flops=COST * pairs * 12 * tokens * 2 * memory * LANES,
            transcendentals=pairs * tokens * 2 * memory,
            bytes_accessed=pairs * LANES * 8 * (tokens + 2 * memory),
        ),
    )(queries, dout, first, second, first, second, first, second, *extra.values())


def split_pairs(total):
    chunks, done, share = [], 0, 0.0
    for shares, turn in CHUNKS:
        start, sizes = done, []
        for s in shares:
            share += s
            end = min(total, round(share * total))
            if end > done:
                sizes.append(end - done)
            done = end
        if sizes:
            chunks.append((start, sizes, turn))
    assert done == total
    return chunks


def solution(mesh):
    n = mesh.shape["ctx"]
    bits = [1 << b for b in range(n.bit_length() - 1)]
    assert n == 1 << len(bits)

    def reduce_order(turn):
        order = list(bits)
        if turn and len(order) > 2:
            order[1], order[2] = order[2], order[1]
        return order

    def swap(x, bit):
        return lax.ppermute(x, "ctx", [(i, i ^ bit) for i in range(n)])

    def gather(x, order):
        for bit in order[:-1]:
            x = jnp.concatenate([x, swap(x, bit)], axis=0)
        return x, swap(x, order[-1])

    def halve(x):
        half = x.shape[0] // 2
        return x[:half], x[half:]

    def per_device(queries, keys, values, lengths, dout):
        rows, width = keys.shape
        live = lax.broadcasted_iota(jnp.int32, (rows, LANES), 0) < lengths[0]
        chunks = split_pairs(width // LANES)
        gathered = []
        for start, sizes, turn in chunks:
            cols = slice(start * LANES, (start + sum(sizes)) * LANES)
            packed = jnp.concatenate([keys[:, cols], values[:, cols], live.astype(BF16)], axis=1)
            gathered.append(gather(packed, reduce_order(turn)[::-1]))
        results, sums, orders = None, [], []
        for (start, sizes, turn), (first, second) in zip(chunks, gathered):
            terms, place, total = None, 0, sum(sizes)
            for size in sizes:
                sent = []
                for j, order in enumerate(orders):
                    if order:
                        if TIE:
                            sums[j], results = lax.optimization_barrier((sums[j], results))
                        keep, send = sums[j] if isinstance(sums[j], (list, tuple)) else halve(sums[j])
                        sent.append((j, keep, swap(send, order.pop(0))))
                out = attention(queries, dout, first, second, results, terms, start + place, place, size, total)
                results, terms = out[:2], out[2:]
                place += size
                for j, keep, received in sent:
                    if TIE:
                        received, results = lax.optimization_barrier((received, results))
                    sums[j] = keep + received
            sums.append(terms)
            orders.append(reduce_order(turn))
        while any(orders):
            for j, order in enumerate(orders):
                if order:
                    keep, send = sums[j] if isinstance(sums[j], (list, tuple)) else halve(sums[j])
                    sums[j] = keep + swap(send, order.pop(0))
        total = jnp.concatenate(sums, axis=1).reshape(rows, width // LANES, 2, LANES)
        key_grad = total[:, :, 0].reshape(rows, width).astype(BF16)
        value_grad = total[:, :, 1].reshape(rows, width).astype(BF16)
        return (*results, key_grad, value_grad)

    spec = P(("groups", "ctx"), None)
    return jax.shard_map(
        per_device,
        mesh=mesh,
        in_specs=(spec, spec, spec, P(("groups", "ctx")), spec),
        out_specs=(spec,) * 4,
        check_vma=False,
    )
```

time: 76.7 us -> 65.9 us (0.86)
  waiting for transfers between devices: 41 us -> 30.3 us
  other arithmetic: 3.43 us -> 0.32 us
  starting transfers between devices: 13 us -> 14.8 us
  local copies, waits for them, and re-layouts: 2.36 us -> 3.15 us
    ppermute x8 -> x16, waiting for transfers between devices: 41 us -> 30.3 us  [swap(): return lax.ppermute(x, 'ctx', [(i, i ^ bit) for i in range(n)])]
    concatenate x3, other arithmetic: 2.41 us -> 0.08 us  [gather(): x = jnp.concatenate([x, swap(x, bit)], axis=0)]
    ppermute x8 -> x16, starting transfers between devices: 13 us -> 14.8 us  [swap(): return lax.ppermute(x, 'ctx', [(i, i ^ bit) for i in range(n)])]
    slice x3 -> x7, local copies, waits for them, and re-layouts: 0.06 us -> 0.85 us  [the longest x1 0.78 us: per_device(): keys[:, cols]]
    concatenate x1, other arithmetic: 0.78 us -> 0.01 us  [per_device(): jnp.concatenate([keys[:, cols], values[:, cols], live.astype(BF16)], axis=1)]
    pallas_call x1 -> x2, Pallas kernels: 15.2 us -> 15.5 us  [attention(): pl.pallas_call(body, grid=(pairs // step,), in_specs=[token_spec, token_s...]
    unnamed x2 -> x4, local copies, waits for them, and re-layouts: 1.59 us -> 1.6 us
  transfers between devices with their start and end apart: 8 -> 16, of which waited for: 8 -> 14; matrix products, arithmetic and copies ran while one was open for 0% -> 0% of each run, Pallas kernels for 0% -> 24%
where the time goes in v2:
time: 65.9 us; the launch traced here: 65.6 us
  waiting for transfers between devices  30.3 us (46%)
  Pallas kernels  15.5 us (24%)
  starting transfers between devices  14.8 us (22%)
  local copies, waits for them, and re-layouts  3.15 us (5%)
  between operations  1.56 us (2%)
    ppermute x16, waiting for transfers between devices, swap(): return lax.ppermute(x, 'ctx', [(i, i ^ bit) for i in range(n)])  30.3 us
    pallas_call x2, Pallas kernels, attention(): pl.pallas_call(body, grid=(pairs // step,), in_specs=[token_spec, token_s...  15.5 us
    ppermute x16, starting transfers between devices, swap(): return lax.ppermute(x, 'ctx', [(i, i ^ bit) for i in range(n)])  14.8 us
    unnamed x4, local copies, waits for them, and re-layouts  1.6 us
  transfers between devices with their start and end apart: 16, of which 14 were waited for; matrix products, arithmetic and copies ran while one was open for 0% of the time, Pallas kernels for 24%

profile of v2, /device:TPU:0, one launch (start us, length us, event | category | flops | bytes accessed | tf_op | source)
XLA Modules:
  0.0 65.6 jit_solution(10786671750613762220)
XLA Ops:
  0.6 0.0 copy-start
  1.4 0.8 %fusion.12 = (bf16[8,1024]{1,0:T(8,128)(2,1)S(1)}, bf16[8,1024]{1,0:T(8,128)(2,1)S(1)}, bf16[8,1024]{1,0:T(8,128)(2,1)S(1)}, bf16[8,1024]{1,0:T(8,128)(2,1)S(1)}) fusion(bf16[8,2048]{1,0:T(8,128)(2,1)} %param.6, bf16[8,2048]{1,0:T(8,128)(2,1)} %param.7), kind=kLoop, calls=%fused_computation.30 | loop fusion | bytes 131072 | tf_op jit(solution)/shard_map/slice | solution.py:151
  2.2 0.1 iota.7
  2.3 4.1 %collective-permute-start = (bf16[8,2176]{1,0:T(8,128)(2,1)S(1)}, bf16[8,2176]{1,0:T(8,128)(2,1)S(1)}, u32[]{:S(2)}, u32[]{:S(2)}) collective-permute-start(bf16[8,2176]{1,0:T(8,128)(2,1)S(1)} %get-tuple-element.33), channel_id=1, source_target_pairs={{0,8},{1,9},{2,10},{3,11},{4,12},{5,13},{6,14},{7,15},{8,0},{9,1},... | collective-permute-start | bytes 104456 | tf_op jit(solution)/shard_map/ppermute | solution.py:133
  6.4 0.1 collective-permute-start.4
  6.4 2.2 %collective-permute-done = bf16[8,2176]{1,0:T(8,128)(2,1)S(1)} collective-permute-done((bf16[8,2176]{1,0:T(8,128)(2,1)S(1)}, bf16[8,2176]{1,0:T(8,128)(2,1)S(1)}, u32[]{:S(2)}, u32[]{:S(2)}) %collective-permute-start) | collective-permute-done | bytes 34848 | tf_op jit(solution)/shard_map/ppermute | solution.py:133
  8.7 2.5 %collective-permute-done.4 = bf16[8,2176]{1,0:T(8,128)(2,1)S(1)} collective-permute-done((bf16[8,2176]{1,0:T(8,128)(2,1)S(1)}, bf16[8,2176]{1,0:T(8,128)(2,1)S(1)}, u32[]{:S(2)}, u32[]{:S(2)}) %collective-permute-start.4) | collective-permute-done | bytes 34848 | tf_op jit(solution)/shard_map/ppermute | solution.py:133
  11.2 1.6 %collective-permute-start.1 = (bf16[16,2176]{1,0:T(8,128)(2,1)S(1)}, bf16[16,2176]{1,0:T(8,128)(2,1)S(1)}, u32[]{:S(2)}, u32[]{:S(2)}) collective-permute-start(bf16[16,2176]{1,0:T(8,128)(2,1)S(1)} %get-tuple-element.31), channel_id=1, source_target_pairs={{0,2},{1,3},{2,0},{3,1},{4,6},{5,7},{6,4},{7,5},{8,10},{9,11},{10,... | collective-permute-start | bytes 208904 | tf_op jit(solution)/shard_map/ppermute | solution.py:133
  12.8 1.6 %collective-permute-start.5 = (bf16[16,2176]{1,0:T(8,128)(2,1)S(1)}, bf16[16,2176]{1,0:T(8,128)(2,1)S(1)}, u32[]{:S(2)}, u32[]{:S(2)}) collective-permute-start(bf16[16,2176]{1,0:T(8,128)(2,1)S(1)} %get-tuple-element.30), channel_id=1, source_target_pairs={{0,4},{1,5},{2,6},{3,7},{4,0},{5,1},{6,2},{7,3},{8,12},{9,13},{10,... | collective-permute-start | bytes 208904 | tf_op jit(solution)/shard_map/ppermute | solution.py:133
  14.4 1.2 %collective-permute-done.1 = bf16[16,2176]{1,0:T(8,128)(2,1)S(1)} collective-permute-done((bf16[16,2176]{1,0:T(8,128)(2,1)S(1)}, bf16[16,2176]{1,0:T(8,128)(2,1)S(1)}, u32[]{:S(2)}, u32[]{:S(2)}) %collective-permute-start.1) | collective-permute-done | bytes 69664 | tf_op jit(solution)/shard_map/ppermute | solution.py:133
  15.6 1.7 %collective-permute-done.5 = bf16[16,2176]{1,0:T(8,128)(2,1)S(1)} collective-permute-done((bf16[16,2176]{1,0:T(8,128)(2,1)S(1)}, bf16[16,2176]{1,0:T(8,128)(2,1)S(1)}, u32[]{:S(2)}, u32[]{:S(2)}) %collective-permute-start.5) | collective-permute-done | bytes 69664 | tf_op jit(solution)/shard_map/ppermute | solution.py:133
  17.3 1.9 %collective-permute-start.2 = (bf16[32,2176]{1,0:T(8,128)(2,1)S(1)}, bf16[32,2176]{1,0:T(8,128)(2,1)S(1)}, u32[]{:S(2)}, u32[]{:S(2)}) collective-permute-start(bf16[32,2176]{1,0:T(8,128)(2,1)S(1)} %get-tuple-element.29), channel_id=1, source_target_pairs={{0,4},{1,5},{2,6},{3,7},{4,0},{5,1},{6,2},{7,3},{8,12},{9,13},{10,... | collective-permute-start | bytes 417800 | tf_op jit(solution)/shard_map/ppermute | solution.py:133
  19.2 0.5 collective-permute-start.6
  19.7 2.7 %collective-permute-done.2 = bf16[32,2176]{1,0:T(8,128)(2,1)S(1)} collective-permute-done((bf16[32,2176]{1,0:T(8,128)(2,1)S(1)}, bf16[32,2176]{1,0:T(8,128)(2,1)S(1)}, u32[]{:S(2)}, u32[]{:S(2)}) %collective-permute-start.2) | collective-permute-done | bytes 139296 | tf_op jit(solution)/shard_map/ppermute | solution.py:133
  22.4 1.8 %collective-permute-done.6 = bf16[32,2176]{1,0:T(8,128)(2,1)S(1)} collective-permute-done((bf16[32,2176]{1,0:T(8,128)(2,1)S(1)}, bf16[32,2176]{1,0:T(8,128)(2,1)S(1)}, u32[]{:S(2)}, u32[]{:S(2)}) %collective-permute-start.6) | collective-permute-done | bytes 139296 | tf_op jit(solution)/shard_map/ppermute | solution.py:133
  24.3 0.1 collective-permute-start.7
  24.4 0.5 collective-permute-start.3
  24.9 1.0 %collective-permute-done.7.refs_3_.refs_5_.refs_7_ = bf16[64,2176]{1,0:T(8,128)(2,1)S(1)} collective-permute-done((bf16[64,2176]{1,0:T(8,128)(2,1)S(1)}, bf16[64,2176]{1,0:T(8,128)(2,1)S(1)}, u32[]{:S(2)}, u32[]{:S(2)}) %collective-permute-start.7) | collective-permute-done | bytes 278560 | tf_op jit(solution)/shard_map/ppermute | solution.py:133
  25.9 0.0 copy-done
  25.9 0.0 copy-start.1
  25.9 1.6 %copy-done.1 = bf16[512,2048]{1,0:T(8,128)(2,1)S(1)} copy-done((bf16[512,2048]{1,0:T(8,128)(2,1)S(1)}, bf16[512,2048]{1,0:T(8,128)(2,1)}, u32[]{:S(2)}) %copy-start.1) | copy-done | bytes 2097176
  27.5 7.8 %shard_map.84 = (bf16[512,2048]{1,0:T(8,128)(2,1)}, bf16[512,2048]{1,0:T(8,128)(2,1)}, f32[64,2048]{1,0:T(8,128)S(1)}, f32[64,2048]{1,0:T(8,128)S(1)}) custom-call(bf16[512,2048]{1,0:T(8,128)(2,1)S(1)} %copy-done, bf16[512,2048]{1,0:T(8,128)(2,1)S(1)} %copy-done.1, bf16[64,2176]{1,0:T(8,128)(2,1)S(1)} %get-tuple-element.26.refs_2_.refs_4_.refs_6_, ...), custom_call_target="tpu_custom_call" | custom-call | flops 1610612736 | bytes 6291456 | tf_op jit(solution)/shard_map/pallas_call | solution.py:85
  35.3 0.1 collective-permute-start.8
  35.4 0.0 collective-permute-done.3.refs_3_.refs_5_.refs_7_
  35.4 7.8 %shard_map.85 = (bf16[512,2048]{1,0:T(8,128)(2,1)}, bf16[512,2048]{1,0:T(8,128)(2,1)}, f32[64,2048]{1,0:T(8,128)S(1)}, f32[64,2048]{1,0:T(8,128)S(1)}) custom-call(bf16[512,2048]{1,0:T(8,128)(2,1)S(1)} %copy-done, bf16[512,2048]{1,0:T(8,128)(2,1)S(1)} %copy-done.1, ...), custom_call_target="tpu_custom_call", output_to_operand_aliasing={{0}: (8, {}), {1}: (9, {})} | custom-call | flops 1610612736 | bytes 6291456 | tf_op jit(solution)/shard_map/pallas_call | solution.py:85
  43.2 0.4 collective-permute-start.12
  43.6 0.0 collective-permute-done.8
  43.6 0.1 add.24
  43.7 0.6 collective-permute-start.9
  44.2 0.9 %collective-permute-done.12 = f32[64,2048]{1,0:T(8,128)S(1)} collective-permute-done((f32[64,2048]{1,0:T(8,128)S(1)}, f32[64,2048]{1,0:T(8,128)S(1)}, u32[]{:S(2)}, u32[]{:S(2)}) %collective-permute-start.12) | collective-permute-done | bytes 524320 | tf_op jit(solution)/shard_map/ppermute | solution.py:133
  45.1 0.1 add.28
  45.2 0.3 collective-permute-start.13
  45.5 6.6 %collective-permute-done.9 = f32[32,2048]{1,0:T(8,128)S(1)} collective-permute-done((f32[32,2048]{1,0:T(8,128)S(1)}, f32[32,2048]{1,0:T(8,128)S(1)}, u32[]{:S(2)}, u32[]{:S(2)}) %collective-permute-start.9) | collective-permute-done | bytes 262176 | tf_op jit(solution)/shard_map/ppermute | solution.py:133
  52.1 0.3 collective-permute-start.10
  52.4 1.4 %collective-permute-done.13 = f32[32,2048]{1,0:T(8,128)S(1)} collective-permute-done((f32[32,2048]{1,0:T(8,128)S(1)}, f32[32,2048]{1,0:T(8,128)S(1)}, u32[]{:S(2)}, u32[]{:S(2)}) %collective-permute-start.13) | collective-permute-done | bytes 262176 | tf_op jit(solution)/shard_map/ppermute | solution.py:133
  53.9 0.6 collective-permute-start.14
  54.5 2.7 %collective-permute-done.10 = f32[16,2048]{1,0:T(8,128)S(1)} collective-permute-done((f32[16,2048]{1,0:T(8,128)S(1)}, f32[16,2048]{1,0:T(8,128)S(1)}, u32[]{:S(2)}, u32[]{:S(2)}) %collective-permute-start.10) | collective-permute-done | bytes 131104 | tf_op jit(solution)/shard_map/ppermute | solution.py:133
  57.2 1.0 %collective-permute-start.11 = (f32[8,2048]{1,0:T(8,128)S(1)}, f32[8,2048]{1,0:T(8,128)S(1)}, u32[]{:S(2)}, u32[]{:S(2)}) collective-permute-start(f32[8,2048]{1,0:T(8,128)S(1)} %slice.79), channel_id=1, source_target_pairs={{0,8},{1,9},{2,10},{3,11},{4,12},{5,13},{6,14},{7,15},{8,0},{9,1},... | collective-permute-start | bytes 196616 | tf_op jit(solution)/shard_map/ppermute | solution.py:133
  58.2 0.7 %collective-permute-done.14 = f32[16,2048]{1,0:T(8,128)S(1)} collective-permute-done((f32[16,2048]{1,0:T(8,128)S(1)}, f32[16,2048]{1,0:T(8,128)S(1)}, u32[]{:S(2)}, u32[]{:S(2)}) %collective-permute-start.14) | collective-permute-done | bytes 131104 | tf_op jit(solution)/shard_map/ppermute | solution.py:133
  59.0 1.3 %collective-permute-start.15 = (f32[8,2048]{1,0:T(8,128)S(1)}, f32[8,2048]{1,0:T(8,128)S(1)}, u32[]{:S(2)}, u32[]{:S(2)}) collective-permute-start(f32[8,2048]{1,0:T(8,128)S(1)} %slice.85), channel_id=1, source_target_pairs={{0,8},{1,9},{2,10},{3,11},{4,12},{5,13},{6,14},{7,15},{8,0},{9,1},... | collective-permute-start | bytes 196616 | tf_op jit(solution)/shard_map/ppermute | solution.py:133
  60.3 4.0 %collective-permute-done.11 = f32[8,2048]{1,0:T(8,128)S(1)} collective-permute-done((f32[8,2048]{1,0:T(8,128)S(1)}, f32[8,2048]{1,0:T(8,128)S(1)}, u32[]{:S(2)}, u32[]{:S(2)}) %collective-permute-start.11) | collective-permute-done | bytes 65568 | tf_op jit(solution)/shard_map/ppermute | solution.py:133
  64.3 0.7 %collective-permute-done.15 = f32[8,2048]{1,0:T(8,128)S(1)} collective-permute-done((f32[8,2048]{1,0:T(8,128)S(1)}, f32[8,2048]{1,0:T(8,128)S(1)}, u32[]{:S(2)}, u32[]{:S(2)}) %collective-permute-start.15) | collective-permute-done | bytes 65568 | tf_op jit(solution)/shard_map/ppermute | solution.py:133
  65.0 0.6 slice_bitcast_fusion
  (18 shorter events, 0.3 us)
Async XLA Ops:
  0.6 25.3 %copy-start = (bf16[512,2048]{1,0:T(8,128)(2,1)S(1)}, bf16[512,2048]{1,0:T(8,128)(2,1)}, u32[]{:S(2)}) copy-start(bf16[512,2048]{1,0:T(8,128)(2,1)} %refs_0_.3) | copy-start | bytes 6291460
  2.3 6.3 %collective-permute-start = (bf16[8,2176]{1,0:T(8,128)(2,1)S(1)}, bf16[8,2176]{1,0:T(8,128)(2,1)S(1)}, u32[]{:S(2)}, u32[]{:S(2)}) collective-permute-start(bf16[8,2176]{1,0:T(8,128)(2,1)S(1)} %get-tuple-element.33), channel_id=1, source_target_pairs={{0,8},{1,9},{2,10},{3,11},{4,12},{5,13},{6,14},{7,15},{8,0},{9,1},... | collective-permute-start | bytes 104456 | tf_op jit(solution)/shard_map/ppermute | solution.py:133
  6.4 4.8 %collective-permute-start.4 = (bf16[8,2176]{1,0:T(8,128)(2,1)S(1)}, bf16[8,2176]{1,0:T(8,128)(2,1)S(1)}, u32[]{:S(2)}, u32[]{:S(2)}) collective-permute-start(bf16[8,2176]{1,0:T(8,128)(2,1)S(1)} %get-tuple-element.32), channel_id=1, source_target_pairs={{0,8},{1,9},{2,10},{3,11},{4,12},{5,13},{6,14},{7,15},{8,0},{9,1},... | collective-permute-start | bytes 104456 | tf_op jit(solution)/shard_map/ppermute | solution.py:133
  11.2 4.4 %collective-permute-start.1 = (bf16[16,2176]{1,0:T(8,128)(2,1)S(1)}, bf16[16,2176]{1,0:T(8,128)(2,1)S(1)}, u32[]{:S(2)}, u32[]{:S(2)}) collective-permute-start(bf16[16,2176]{1,0:T(8,128)(2,1)S(1)} %get-tuple-element.31), channel_id=1, source_target_pairs={{0,2},{1,3},{2,0},{3,1},{4,6},{5,7},{6,4},{7,5},{8,10},{9,11},{10,... | collective-permute-start | bytes 208904 | tf_op jit(solution)/shard_map/ppermute | solution.py:133
  12.8 4.5 %collective-permute-start.5 = (bf16[16,2176]{1,0:T(8,128)(2,1)S(1)}, bf16[16,2176]{1,0:T(8,128)(2,1)S(1)}, u32[]{:S(2)}, u32[]{:S(2)}) collective-permute-start(bf16[16,2176]{1,0:T(8,128)(2,1)S(1)} %get-tuple-element.30), channel_id=1, source_target_pairs={{0,4},{1,5},{2,6},{3,7},{4,0},{5,1},{6,2},{7,3},{8,12},{9,13},{10,... | collective-permute-start | bytes 208904 | tf_op jit(solution)/shard_map/ppermute | solution.py:133
  17.3 5.1 %collective-permute-start.2 = (bf16[32,2176]{1,0:T(8,128)(2,1)S(1)}, bf16[32,2176]{1,0:T(8,128)(2,1)S(1)}, u32[]{:S(2)}, u32[]{:S(2)}) collective-permute-start(bf16[32,2176]{1,0:T(8,128)(2,1)S(1)} %get-tuple-element.29), channel_id=1, source_target_pairs={{0,4},{1,5},{2,6},{3,7},{4,0},{5,1},{6,2},{7,3},{8,12},{9,13},{10,... | collective-permute-start | bytes 417800 | tf_op jit(solution)/shard_map/ppermute | solution.py:133
  19.2 5.1 %collective-permute-start.6 = (bf16[32,2176]{1,0:T(8,128)(2,1)S(1)}, bf16[32,2176]{1,0:T(8,128)(2,1)S(1)}, u32[]{:S(2)}, u32[]{:S(2)}) collective-permute-start(bf16[32,2176]{1,0:T(8,128)(2,1)S(1)} %get-tuple-element.28), channel_id=1, source_target_pairs={{0,2},{1,3},{2,0},{3,1},{4,6},{5,7},{6,4},{7,5},{8,10},{9,11},{10,... | collective-permute-start | bytes 417800 | tf_op jit(solution)/shard_map/ppermute | solution.py:133
  24.3 1.6 %collective-permute-start.7 = (bf16[64,2176]{1,0:T(8,128)(2,1)S(1)}, bf16[64,2176]{1,0:T(8,128)(2,1)S(1)}, u32[]{:S(2)}, u32[]{:S(2)}) collective-permute-start(bf16[64,2176]{1,0:T(8,128)(2,1)S(1)} %get-tuple-element.26.refs_2_.refs_4_.refs_6_), channel_id=1, source_target_pairs={{0,1},{1,0},{2,3},{3,2},{4,5},{5,4},{6,7},{7,6},{8,9},{9,8},{10,11... | collective-permute-start | bytes 835592 | tf_op jit(solution)/shard_map/ppermute | solution.py:133
  24.4 11.0 %collective-permute-start.3 = (bf16[64,2176]{1,0:T(8,128)(2,1)S(1)}, bf16[64,2176]{1,0:T(8,128)(2,1)S(1)}, u32[]{:S(2)}, u32[]{:S(2)}) collective-permute-start(bf16[64,2176]{1,0:T(8,128)(2,1)S(1)} %get-tuple-element.27.refs_2_.refs_4_.refs_6_), channel_id=1, source_target_pairs={{0,1},{1,0},{2,3},{3,2},{4,5},{5,4},{6,7},{7,6},{8,9},{9,8},{10,11... | collective-permute-start | bytes 835592 | tf_op jit(solution)/shard_map/ppermute | solution.py:133
  25.9 1.6 %copy-start.1 = (bf16[512,2048]{1,0:T(8,128)(2,1)S(1)}, bf16[512,2048]{1,0:T(8,128)(2,1)}, u32[]{:S(2)}) copy-start(bf16[512,2048]{1,0:T(8,128)(2,1)} %refs_1_.3) | copy-start | bytes 6291460
  35.3 8.3 %collective-permute-start.8 = (f32[64,2048]{1,0:T(8,128)S(1)}, f32[64,2048]{1,0:T(8,128)S(1)}, u32[]{:S(2)}, u32[]{:S(2)}) collective-permute-start(f32[64,2048]{1,0:T(8,128)S(1)} %get-tuple-element.17), channel_id=1, source_target_pairs={{0,1},{1,0},{2,3},{3,2},{4,5},{5,4},{6,7},{7,6},{8,9},{9,8},{10,11... | collective-permute-start | bytes 1572872 | tf_op jit(solution)/shard_map/ppermute | solution.py:133
  43.2 1.9 %collective-permute-start.12 = (f32[64,2048]{1,0:T(8,128)S(1)}, f32[64,2048]{1,0:T(8,128)S(1)}, u32[]{:S(2)}, u32[]{:S(2)}) collective-permute-start(f32[64,2048]{1,0:T(8,128)S(1)} %get-tuple-element.19), channel_id=1, source_target_pairs={{0,1},{1,0},{2,3},{3,2},{4,5},{5,4},{6,7},{7,6},{8,9},{9,8},{10,11... | collective-permute-start | bytes 1572872 | tf_op jit(solution)/shard_map/ppermute | solution.py:133
  43.7 8.4 %collective-permute-start.9 = (f32[32,2048]{1,0:T(8,128)S(1)}, f32[32,2048]{1,0:T(8,128)S(1)}, u32[]{:S(2)}, u32[]{:S(2)}) collective-permute-start(f32[32,2048]{1,0:T(8,128)S(1)} %slice.75), channel_id=1, source_target_pairs={{0,2},{1,3},{2,0},{3,1},{4,6},{5,7},{6,4},{7,5},{8,10},{9,11},{10,... | collective-permute-start | bytes 786440 | tf_op jit(solution)/shard_map/ppermute | solution.py:133
  45.2 8.7 %collective-permute-start.13 = (f32[32,2048]{1,0:T(8,128)S(1)}, f32[32,2048]{1,0:T(8,128)S(1)}, u32[]{:S(2)}, u32[]{:S(2)}) collective-permute-start(f32[32,2048]{1,0:T(8,128)S(1)} %slice.81), channel_id=1, source_target_pairs={{0,4},{1,5},{2,6},{3,7},{4,0},{5,1},{6,2},{7,3},{8,12},{9,13},{10,... | collective-permute-start | bytes 786440 | tf_op jit(solution)/shard_map/ppermute | solution.py:133
  52.1 5.0 %collective-permute-start.10 = (f32[16,2048]{1,0:T(8,128)S(1)}, f32[16,2048]{1,0:T(8,128)S(1)}, u32[]{:S(2)}, u32[]{:S(2)}) collective-permute-start(f32[16,2048]{1,0:T(8,128)S(1)} %slice.77), channel_id=1, source_target_pairs={{0,4},{1,5},{2,6},{3,7},{4,0},{5,1},{6,2},{7,3},{8,12},{9,13},{10,... | collective-permute-start | bytes 393224 | tf_op jit(solution)/shard_map/ppermute | solution.py:133
  53.9 5.0 %collective-permute-start.14 = (f32[16,2048]{1,0:T(8,128)S(1)}, f32[16,2048]{1,0:T(8,128)S(1)}, u32[]{:S(2)}, u32[]{:S(2)}) collective-permute-start(f32[16,2048]{1,0:T(8,128)S(1)} %slice.83), channel_id=1, source_target_pairs={{0,2},{1,3},{2,0},{3,1},{4,6},{5,7},{6,4},{7,5},{8,10},{9,11},{10,... | collective-permute-start | bytes 393224 | tf_op jit(solution)/shard_map/ppermute | solution.py:133
  57.2 7.1 %collective-permute-start.11 = (f32[8,2048]{1,0:T(8,128)S(1)}, f32[8,2048]{1,0:T(8,128)S(1)}, u32[]{:S(2)}, u32[]{:S(2)}) collective-permute-start(f32[8,2048]{1,0:T(8,128)S(1)} %slice.79), channel_id=1, source_target_pairs={{0,8},{1,9},{2,10},{3,11},{4,12},{5,13},{6,14},{7,15},{8,0},{9,1},... | collective-permute-start | bytes 196616 | tf_op jit(solution)/shard_map/ppermute | solution.py:133
  59.0 6.0 %collective-permute-start.15 = (f32[8,2048]{1,0:T(8,128)S(1)}, f32[8,2048]{1,0:T(8,128)S(1)}, u32[]{:S(2)}, u32[]{:S(2)}) collective-permute-start(f32[8,2048]{1,0:T(8,128)S(1)} %slice.85), channel_id=1, source_target_pairs={{0,8},{1,9},{2,10},{3,11},{4,12},{5,13},{6,14},{7,15},{8,0},{9,1},... | collective-permute-start | bytes 196616 | tf_op jit(solution)/shard_map/ppermute | solution.py:133

commit v3 on v2

--- a/solution.py
+++ b/solution.py
@@ -36,10 +36,11 @@
     return att.T, dq.T, dot(grad_s, q, 1, 0), dot(p_low, do, 1, 0)
 
 
-def attention(queries, dout, first, second, results, terms, offset, place, pairs, total):
+def attention(queries, dout, first, second, live, order, results, terms, offset, place, pairs, total):
     tokens, width = queries.shape
     half = first.shape[0]
     memory = 2 * half
+    rows = memory // len(order)
     most = max(1, PAIRS_PER_STEP * 128 // memory)
     step = max(d for d in range(1, most + 1) if all(x % d == 0 for x in (pairs, offset, place, total)))
     block = step * LANES
@@ -47,8 +48,9 @@
     def body(*refs):
         q_ref, do_ref, ka_ref, kb_ref, va_ref, vb_ref, fa_ref, fb_ref = refs[:8]
         att_ref, dq_ref, lo_ref, hi_ref = refs[-4:]
-        live = jnp.concatenate([fa_ref[...], fb_ref[...]], axis=0).astype(F32)
-        bias = jnp.where(live[:, :1] > 0, 0.0, NEG)
+        flags = jnp.concatenate([fa_ref[...], fb_ref[...]], axis=0).astype(F32)
+        flags = jnp.concatenate([flags[at * rows : (at + 1) * rows, :1] for at in order], axis=0)
+        bias = jnp.where(flags > 0, 0.0, NEG)
         left = lax.broadcasted_iota(jnp.int32, (memory, LANES), 1) < HEAD_DIM
         zero = jnp.zeros((memory, LANES), BF16)
 
@@ -74,7 +76,7 @@
     token_spec = cols(tokens, block, offset // step)
     k_spec = cols(half, block, place // step)
     v_spec = cols(half, block, (total + place) // step)
-    flag_spec = pl.BlockSpec((half, LANES), lambda g: (0, 2 * total))
+    flag_spec = pl.BlockSpec((half, LANES), lambda g: (0, live[0].shape[1] // LANES - 1))
     term_spec = cols(half, 2 * block, place // step)
     extra = {}
     if results is not None:
@@ -99,7 +101,7 @@
             transcendentals=pairs * tokens * 2 * memory,
             bytes_accessed=pairs * LANES * 8 * (tokens + 2 * memory),
         ),
-    )(queries, dout, first, second, first, second, first, second, *extra.values())
+    )(queries, dout, first, second, first, second, *live, *extra.values())
 
 
 def split_pairs(total):
@@ -137,6 +139,9 @@
             x = jnp.concatenate([x, swap(x, bit)], axis=0)
         return x, swap(x, order[-1])
 
+    def places(order):
+        return [sum(b for i, b in enumerate(order) if j >> i & 1) for j in range(n)]
+
     def halve(x):
         half = x.shape[0] // 2
         return x[:half], x[half:]
@@ -148,11 +153,13 @@
         gathered = []
         for start, sizes, turn in chunks:
             cols = slice(start * LANES, (start + sum(sizes)) * LANES)
-            packed = jnp.concatenate([keys[:, cols], values[:, cols], live.astype(BF16)], axis=1)
-            gathered.append(gather(packed, reduce_order(turn)[::-1]))
+            packed = [keys[:, cols], values[:, cols]] + ([] if gathered else [live.astype(BF16)])
+            gathered.append(gather(jnp.concatenate(packed, axis=1), reduce_order(turn)[::-1]))
+        flag_places = places(reduce_order(chunks[0][2])[::-1])
         results, sums, orders = None, [], []
         for (start, sizes, turn), (first, second) in zip(chunks, gathered):
             terms, place, total = None, 0, sum(sizes)
+            at = [flag_places.index(p) for p in places(reduce_order(turn)[::-1])]
             for size in sizes:
                 sent = []
                 for j, order in enumerate(orders):
@@ -161,7 +168,9 @@
                             sums[j], results = lax.optimization_barrier((sums[j], results))
                         keep, send = sums[j] if isinstance(sums[j], (list, tuple)) else halve(sums[j])
                         sent.append((j, keep, swap(send, order.pop(0))))
-                out = attention(queries, dout, first, second, results, terms, start + place, place, size, total)
+                out = attention(
+                    queries, dout, first, second, gathered[0], at, results, terms, start + place, place, size, total
+                )
                 results, terms = out[:2], out[2:]
                 place += size
                 for j, keep, received in sent:

time: 65.9 us -> 62.3 us (0.945)
  waiting for transfers between devices: 30.3 us -> 20.9 us
  starting transfers between devices: 14.8 us -> 20.7 us
    ppermute x16, waiting for transfers between devices: 30.3 us -> 20.9 us  [swap(): return lax.ppermute(x, 'ctx', [(i, i ^ bit) for i in range(n)])]
    ppermute x16, starting transfers between devices: 14.8 us -> 20.7 us  [swap(): return lax.ppermute(x, 'ctx', [(i, i ^ bit) for i in range(n)])]
  transfers between devices with their start and end apart: 16 -> 16, of which waited for: 14 -> 11; matrix products, arithmetic and copies ran while one was open for 0% -> 1% of each run, Pallas kernels for 24% -> 25%
where the time goes in v3:
time: 62.3 us; the launch traced here: 62 us
  waiting for transfers between devices  20.9 us (34%)
  starting transfers between devices  20.7 us (33%)
  Pallas kernels  15.3 us (25%)
  local copies, waits for them, and re-layouts  3.14 us (5%)
  between operations  1.58 us (3%)
    ppermute x16, waiting for transfers between devices, swap(): return lax.ppermute(x, 'ctx', [(i, i ^ bit) for i in range(n)])  20.9 us
    ppermute x16, starting transfers between devices, swap(): return lax.ppermute(x, 'ctx', [(i, i ^ bit) for i in range(n)])  20.7 us
    pallas_call x2, Pallas kernels, attention(): pl.pallas_call(body, grid=(pairs // step,), in_specs=[token_spec, token_s...  15.3 us
    unnamed x4, local copies, waits for them, and re-layouts  1.59 us
  transfers between devices with their start and end apart: 16, of which 11 were waited for; matrix products, arithmetic and copies ran while one was open for 1% of the time, Pallas kernels for 25%

profile of v3, /device:TPU:0, one launch (start us, length us, event | category | flops | bytes accessed | tf_op | source)
XLA Modules:
  0.0 62.0 jit_solution(10037207483086225691)
XLA Ops:
  0.6 0.0 copy-start
  1.4 0.8 %fusion = (bf16[8,1024]{1,0:T(8,128)(2,1)S(1)}, bf16[8,1024]{1,0:T(8,128)(2,1)S(1)}, bf16[8,1024]{1,0:T(8,128)(2,1)S(1)}, bf16[8,1024]{1,0:T(8,128)(2,1)S(1)}) fusion(bf16[8,2048]{1,0:T(8,128)(2,1)} %param.6, bf16[8,2048]{1,0:T(8,128)(2,1)} %param.7), kind=kLoop, calls=%fused_computation.18 | loop fusion | bytes 131072 | tf_op jit(solution)/shard_map/slice | solution.py:156
  2.2 0.1 iota.7
  2.3 4.0 %collective-permute-start.4 = (bf16[8,2176]{1,0:T(8,128)(2,1)S(1)}, bf16[8,2176]{1,0:T(8,128)(2,1)S(1)}, u32[]{:S(2)}, u32[]{:S(2)}) collective-permute-start(bf16[8,2176]{1,0:T(8,128)(2,1)S(1)} %pad_maximum_fusion.6), channel_id=1, source_target_pairs={{0,8},{1,9},{2,10},{3,11},{4,12},{5,13},{6,14},{7,15},{8,0},{9,1},... | collective-permute-start | bytes 104456 | tf_op jit(solution)/shard_map/ppermute | solution.py:135
  6.4 0.1 collective-permute-start
  6.4 2.2 %collective-permute-done.4 = bf16[8,2176]{1,0:T(8,128)(2,1)S(1)} collective-permute-done((bf16[8,2176]{1,0:T(8,128)(2,1)S(1)}, bf16[8,2176]{1,0:T(8,128)(2,1)S(1)}, u32[]{:S(2)}, u32[]{:S(2)}) %collective-permute-start.4) | collective-permute-done | bytes 34848 | tf_op jit(solution)/shard_map/ppermute | solution.py:135
  8.6 1.7 %collective-permute-start.5 = (bf16[16,2176]{1,0:T(8,128)(2,1)S(1)}, bf16[16,2176]{1,0:T(8,128)(2,1)S(1)}, u32[]{:S(2)}, u32[]{:S(2)}) collective-permute-start(bf16[16,2176]{1,0:T(8,128)(2,1)S(1)} %pad_maximum_fusion.4), channel_id=1, source_target_pairs={{0,4},{1,5},{2,6},{3,7},{4,0},{5,1},{6,2},{7,3},{8,12},{9,13},{10,... | collective-permute-start | bytes 208904 | tf_op jit(solution)/shard_map/ppermute | solution.py:135
  10.3 0.8 %collective-permute-done = bf16[8,2048]{1,0:T(8,128)(2,1)S(1)} collective-permute-done((bf16[8,2048]{1,0:T(8,128)(2,1)S(1)}, bf16[8,2048]{1,0:T(8,128)(2,1)S(1)}, u32[]{:S(2)}, u32[]{:S(2)}) %collective-permute-start) | collective-permute-done | bytes 32800 | tf_op jit(solution)/shard_map/ppermute | solution.py:135
  11.2 1.5 %collective-permute-start.1 = (bf16[16,2048]{1,0:T(8,128)(2,1)S(1)}, bf16[16,2048]{1,0:T(8,128)(2,1)S(1)}, u32[]{:S(2)}, u32[]{:S(2)}) collective-permute-start(bf16[16,2048]{1,0:T(8,128)(2,1)S(1)} %pad_maximum_fusion.5), channel_id=1, source_target_pairs={{0,2},{1,3},{2,0},{3,1},{4,6},{5,7},{6,4},{7,5},{8,10},{9,11},{10,... | collective-permute-start | bytes 196616 | tf_op jit(solution)/shard_map/ppermute | solution.py:135
  12.7 0.3 collective-permute-done.5
  13.0 1.8 %collective-permute-start.6 = (bf16[32,2176]{1,0:T(8,128)(2,1)S(1)}, bf16[32,2176]{1,0:T(8,128)(2,1)S(1)}, u32[]{:S(2)}, u32[]{:S(2)}) collective-permute-start(bf16[32,2176]{1,0:T(8,128)(2,1)S(1)} %pad_maximum_fusion.2), channel_id=1, source_target_pairs={{0,2},{1,3},{2,0},{3,1},{4,6},{5,7},{6,4},{7,5},{8,10},{9,11},{10,... | collective-permute-start | bytes 417800 | tf_op jit(solution)/shard_map/ppermute | solution.py:135
  14.8 1.1 %collective-permute-done.1 = bf16[16,2048]{1,0:T(8,128)(2,1)S(1)} collective-permute-done((bf16[16,2048]{1,0:T(8,128)(2,1)S(1)}, bf16[16,2048]{1,0:T(8,128)(2,1)S(1)}, u32[]{:S(2)}, u32[]{:S(2)}) %collective-permute-start.1) | collective-permute-done | bytes 65568 | tf_op jit(solution)/shard_map/ppermute | solution.py:135
  15.9 1.5 %collective-permute-start.2 = (bf16[32,2048]{1,0:T(8,128)(2,1)S(1)}, bf16[32,2048]{1,0:T(8,128)(2,1)S(1)}, u32[]{:S(2)}, u32[]{:S(2)}) collective-permute-start(bf16[32,2048]{1,0:T(8,128)(2,1)S(1)} %pad_maximum_fusion.3), channel_id=1, source_target_pairs={{0,4},{1,5},{2,6},{3,7},{4,0},{5,1},{6,2},{7,3},{8,12},{9,13},{10,... | collective-permute-start | bytes 393224 | tf_op jit(solution)/shard_map/ppermute | solution.py:135
  17.4 0.7 %collective-permute-done.6 = bf16[32,2176]{1,0:T(8,128)(2,1)S(1)} collective-permute-done((bf16[32,2176]{1,0:T(8,128)(2,1)S(1)}, bf16[32,2176]{1,0:T(8,128)(2,1)S(1)}, u32[]{:S(2)}, u32[]{:S(2)}) %collective-permute-start.6) | collective-permute-done | bytes 139296 | tf_op jit(solution)/shard_map/ppermute | solution.py:135
  18.1 0.1 collective-permute-start.7
  18.2 2.8 %collective-permute-done.2 = bf16[32,2048]{1,0:T(8,128)(2,1)S(1)} collective-permute-done((bf16[32,2048]{1,0:T(8,128)(2,1)S(1)}, bf16[32,2048]{1,0:T(8,128)(2,1)S(1)}, u32[]{:S(2)}, u32[]{:S(2)}) %collective-permute-start.2) | collective-permute-done | bytes 131104 | tf_op jit(solution)/shard_map/ppermute | solution.py:135
  21.0 0.1 collective-permute-start.3
  21.1 0.0 collective-permute-done.7.refs_3_.refs_5_.refs_7_
  21.1 0.0 copy-done
  21.1 0.0 copy-start.1
  21.1 1.6 %copy-done.1 = bf16[512,2048]{1,0:T(8,128)(2,1)S(1)} copy-done((bf16[512,2048]{1,0:T(8,128)(2,1)S(1)}, bf16[512,2048]{1,0:T(8,128)(2,1)}, u32[]{:S(2)}) %copy-start.1) | copy-done | bytes 2097176
  22.7 7.8 %shard_map.84 = (bf16[512,2048]{1,0:T(8,128)(2,1)}, bf16[512,2048]{1,0:T(8,128)(2,1)}, f32[64,2048]{1,0:T(8,128)S(1)}, f32[64,2048]{1,0:T(8,128)S(1)}) custom-call(bf16[512,2048]{1,0:T(8,128)(2,1)S(1)} %copy-done, bf16[512,2048]{1,0:T(8,128)(2,1)S(1)} %copy-done.1, bf16[64,2176]{1,0:T(8,128)(2,1)S(1)} %pad_maximum_fusion.refs_2_.refs_4_.refs_6_, ...), custom_call_target="tpu_custom_call" | custom-call | flops 1610612736 | bytes 6291456 | tf_op jit(solution)/shard_map/pallas_call | solution.py:87
  30.4 0.5 collective-permute-start.8
  30.9 0.0 collective-permute-done.3.refs_3_.refs_5_
  30.9 7.5 %shard_map.85 = (bf16[512,2048]{1,0:T(8,128)(2,1)}, bf16[512,2048]{1,0:T(8,128)(2,1)}, f32[64,2048]{1,0:T(8,128)S(1)}, f32[64,2048]{1,0:T(8,128)S(1)}) custom-call(bf16[512,2048]{1,0:T(8,128)(2,1)S(1)} %copy-done, bf16[512,2048]{1,0:T(8,128)(2,1)S(1)} %copy-done.1, ...), custom_call_target="tpu_custom_call", output_to_operand_aliasing={{0}: (8, {}), {1}: (9, {})} | custom-call | flops 1610612736 | bytes 6291456 | tf_op jit(solution)/shard_map/pallas_call | solution.py:87
  38.4 0.0 collective-permute-start.12
  38.5 0.0 collective-permute-done.8
  38.5 0.1 add.24
  38.6 1.1 %collective-permute-start.9 = (f32[32,2048]{1,0:T(8,128)S(1)}, f32[32,2048]{1,0:T(8,128)S(1)}, u32[]{:S(2)}, u32[]{:S(2)}) collective-permute-start(f32[32,2048]{1,0:T(8,128)S(1)} %slice.75), channel_id=1, source_target_pairs={{0,2},{1,3},{2,0},{3,1},{4,6},{5,7},{6,4},{7,5},{8,10},{9,11},{10,... | collective-permute-start | bytes 786440 | tf_op jit(solution)/shard_map/ppermute | solution.py:135
  39.7 0.7 %collective-permute-done.12 = f32[64,2048]{1,0:T(8,128)S(1)} collective-permute-done((f32[64,2048]{1,0:T(8,128)S(1)}, f32[64,2048]{1,0:T(8,128)S(1)}, u32[]{:S(2)}, u32[]{:S(2)}) %collective-permute-start.12) | collective-permute-done | bytes 524320 | tf_op jit(solution)/shard_map/ppermute | solution.py:135
  40.3 0.1 add.28
  40.4 1.4 %collective-permute-start.13 = (f32[32,2048]{1,0:T(8,128)S(1)}, f32[32,2048]{1,0:T(8,128)S(1)}, u32[]{:S(2)}, u32[]{:S(2)}) collective-permute-start(f32[32,2048]{1,0:T(8,128)S(1)} %slice.81), channel_id=1, source_target_pairs={{0,4},{1,5},{2,6},{3,7},{4,0},{5,1},{6,2},{7,3},{8,12},{9,13},{10,... | collective-permute-start | bytes 786440 | tf_op jit(solution)/shard_map/ppermute | solution.py:135
  41.9 5.4 %collective-permute-done.9 = f32[32,2048]{1,0:T(8,128)S(1)} collective-permute-done((f32[32,2048]{1,0:T(8,128)S(1)}, f32[32,2048]{1,0:T(8,128)S(1)}, u32[]{:S(2)}, u32[]{:S(2)}) %collective-permute-start.9) | collective-permute-done | bytes 262176 | tf_op jit(solution)/shard_map/ppermute | solution.py:135
  47.4 1.4 %collective-permute-start.10 = (f32[16,2048]{1,0:T(8,128)S(1)}, f32[16,2048]{1,0:T(8,128)S(1)}, u32[]{:S(2)}, u32[]{:S(2)}) collective-permute-start(f32[16,2048]{1,0:T(8,128)S(1)} %slice.77), channel_id=1, source_target_pairs={{0,4},{1,5},{2,6},{3,7},{4,0},{5,1},{6,2},{7,3},{8,12},{9,13},{10,... | collective-permute-start | bytes 393224 | tf_op jit(solution)/shard_map/ppermute | solution.py:135
  48.8 0.0 collective-permute-done.13
  48.9 1.6 %collective-permute-start.14 = (f32[16,2048]{1,0:T(8,128)S(1)}, f32[16,2048]{1,0:T(8,128)S(1)}, u32[]{:S(2)}, u32[]{:S(2)}) collective-permute-start(f32[16,2048]{1,0:T(8,128)S(1)} %slice.83), channel_id=1, source_target_pairs={{0,2},{1,3},{2,0},{3,1},{4,6},{5,7},{6,4},{7,5},{8,10},{9,11},{10,... | collective-permute-start | bytes 393224 | tf_op jit(solution)/shard_map/ppermute | solution.py:135
  50.5 2.0 %collective-permute-done.10 = f32[16,2048]{1,0:T(8,128)S(1)} collective-permute-done((f32[16,2048]{1,0:T(8,128)S(1)}, f32[16,2048]{1,0:T(8,128)S(1)}, u32[]{:S(2)}, u32[]{:S(2)}) %collective-permute-start.10) | collective-permute-done | bytes 131104 | tf_op jit(solution)/shard_map/ppermute | solution.py:135
  52.6 2.5 %collective-permute-start.11 = (f32[8,2048]{1,0:T(8,128)S(1)}, f32[8,2048]{1,0:T(8,128)S(1)}, u32[]{:S(2)}, u32[]{:S(2)}) collective-permute-start(f32[8,2048]{1,0:T(8,128)S(1)} %slice.79), channel_id=1, source_target_pairs={{0,8},{1,9},{2,10},{3,11},{4,12},{5,13},{6,14},{7,15},{8,0},{9,1},... | collective-permute-start | bytes 196616 | tf_op jit(solution)/shard_map/ppermute | solution.py:135
  55.1 0.0 collective-permute-done.14
  55.1 1.4 %collective-permute-start.15 = (f32[8,2048]{1,0:T(8,128)S(1)}, f32[8,2048]{1,0:T(8,128)S(1)}, u32[]{:S(2)}, u32[]{:S(2)}) collective-permute-start(f32[8,2048]{1,0:T(8,128)S(1)} %slice.85), channel_id=1, source_target_pairs={{0,8},{1,9},{2,10},{3,11},{4,12},{5,13},{6,14},{7,15},{8,0},{9,1},... | collective-permute-start | bytes 196616 | tf_op jit(solution)/shard_map/ppermute | solution.py:135
  56.5 3.3 %collective-permute-done.11 = f32[8,2048]{1,0:T(8,128)S(1)} collective-permute-done((f32[8,2048]{1,0:T(8,128)S(1)}, f32[8,2048]{1,0:T(8,128)S(1)}, u32[]{:S(2)}, u32[]{:S(2)}) %collective-permute-start.11) | collective-permute-done | bytes 65568 | tf_op jit(solution)/shard_map/ppermute | solution.py:135
  59.8 1.5 %collective-permute-done.15 = f32[8,2048]{1,0:T(8,128)S(1)} collective-permute-done((f32[8,2048]{1,0:T(8,128)S(1)}, f32[8,2048]{1,0:T(8,128)S(1)}, u32[]{:S(2)}, u32[]{:S(2)}) %collective-permute-start.15) | collective-permute-done | bytes 65568 | tf_op jit(solution)/shard_map/ppermute | solution.py:135
  61.3 0.6 %slice_bitcast_fusion = (bf16[8,2048]{1,0:T(8,128)(2,1)}, bf16[8,2048]{1,0:T(8,128)(2,1)}) fusion(bf16[8,16,2,128]{3,0,2,1:T(8,128)(2,1)S(1)} %bitcast.7), kind=kLoop, calls=%fused_computation.14 | loop fusion | bytes 131072 | tf_op jit(solution)/shard_map/convert_element_type | solution.py:189
  (22 shorter events, 0.3 us)
Async XLA Ops:
  0.6 20.4 %copy-start = (bf16[512,2048]{1,0:T(8,128)(2,1)S(1)}, bf16[512,2048]{1,0:T(8,128)(2,1)}, u32[]{:S(2)}) copy-start(bf16[512,2048]{1,0:T(8,128)(2,1)} %refs_0_.3) | copy-start | bytes 6291460
  2.3 6.3 %collective-permute-start.4 = (bf16[8,2176]{1,0:T(8,128)(2,1)S(1)}, bf16[8,2176]{1,0:T(8,128)(2,1)S(1)}, u32[]{:S(2)}, u32[]{:S(2)}) collective-permute-start(bf16[8,2176]{1,0:T(8,128)(2,1)S(1)} %pad_maximum_fusion.6), channel_id=1, source_target_pairs={{0,8},{1,9},{2,10},{3,11},{4,12},{5,13},{6,14},{7,15},{8,0},{9,1},... | collective-permute-start | bytes 104456 | tf_op jit(solution)/shard_map/ppermute | solution.py:135
  6.4 4.8 %collective-permute-start = (bf16[8,2048]{1,0:T(8,128)(2,1)S(1)}, bf16[8,2048]{1,0:T(8,128)(2,1)S(1)}, u32[]{:S(2)}, u32[]{:S(2)}) collective-permute-start(bf16[8,2048]{1,0:T(8,128)(2,1)S(1)} %pad_maximum_fusion.7), channel_id=1, source_target_pairs={{0,8},{1,9},{2,10},{3,11},{4,12},{5,13},{6,14},{7,15},{8,0},{9,1},... | collective-permute-start | bytes 98312 | tf_op jit(solution)/shard_map/ppermute | solution.py:135
  8.6 4.3 %collective-permute-start.5 = (bf16[16,2176]{1,0:T(8,128)(2,1)S(1)}, bf16[16,2176]{1,0:T(8,128)(2,1)S(1)}, u32[]{:S(2)}, u32[]{:S(2)}) collective-permute-start(bf16[16,2176]{1,0:T(8,128)(2,1)S(1)} %pad_maximum_fusion.4), channel_id=1, source_target_pairs={{0,4},{1,5},{2,6},{3,7},{4,0},{5,1},{6,2},{7,3},{8,12},{9,13},{10,... | collective-permute-start | bytes 208904 | tf_op jit(solution)/shard_map/ppermute | solution.py:135
  11.2 4.7 %collective-permute-start.1 = (bf16[16,2048]{1,0:T(8,128)(2,1)S(1)}, bf16[16,2048]{1,0:T(8,128)(2,1)S(1)}, u32[]{:S(2)}, u32[]{:S(2)}) collective-permute-start(bf16[16,2048]{1,0:T(8,128)(2,1)S(1)} %pad_maximum_fusion.5), channel_id=1, source_target_pairs={{0,2},{1,3},{2,0},{3,1},{4,6},{5,7},{6,4},{7,5},{8,10},{9,11},{10,... | collective-permute-start | bytes 196616 | tf_op jit(solution)/shard_map/ppermute | solution.py:135
  13.0 5.1 %collective-permute-start.6 = (bf16[32,2176]{1,0:T(8,128)(2,1)S(1)}, bf16[32,2176]{1,0:T(8,128)(2,1)S(1)}, u32[]{:S(2)}, u32[]{:S(2)}) collective-permute-start(bf16[32,2176]{1,0:T(8,128)(2,1)S(1)} %pad_maximum_fusion.2), channel_id=1, source_target_pairs={{0,2},{1,3},{2,0},{3,1},{4,6},{5,7},{6,4},{7,5},{8,10},{9,11},{10,... | collective-permute-start | bytes 417800 | tf_op jit(solution)/shard_map/ppermute | solution.py:135
  15.9 5.0 %collective-permute-start.2 = (bf16[32,2048]{1,0:T(8,128)(2,1)S(1)}, bf16[32,2048]{1,0:T(8,128)(2,1)S(1)}, u32[]{:S(2)}, u32[]{:S(2)}) collective-permute-start(bf16[32,2048]{1,0:T(8,128)(2,1)S(1)} %pad_maximum_fusion.3), channel_id=1, source_target_pairs={{0,4},{1,5},{2,6},{3,7},{4,0},{5,1},{6,2},{7,3},{8,12},{9,13},{10,... | collective-permute-start | bytes 393224 | tf_op jit(solution)/shard_map/ppermute | solution.py:135
  18.1 2.9 %collective-permute-start.7 = (bf16[64,2176]{1,0:T(8,128)(2,1)S(1)}, bf16[64,2176]{1,0:T(8,128)(2,1)S(1)}, u32[]{:S(2)}, u32[]{:S(2)}) collective-permute-start(bf16[64,2176]{1,0:T(8,128)(2,1)S(1)} %pad_maximum_fusion.refs_2_.refs_4_.refs_6_), channel_id=1, source_target_pairs={{0,1},{1,0},{2,3},{3,2},{4,5},{5,4},{6,7},{7,6},{8,9},{9,8},{10,11... | collective-permute-start | bytes 835592 | tf_op jit(solution)/shard_map/ppermute | solution.py:135
  21.0 9.9 %collective-permute-start.3 = (bf16[64,2048]{1,0:T(8,128)(2,1)S(1)}, bf16[64,2048]{1,0:T(8,128)(2,1)S(1)}, u32[]{:S(2)}, u32[]{:S(2)}) collective-permute-start(bf16[64,2048]{1,0:T(8,128)(2,1)S(1)} %pad_maximum_fusion.1.refs_2_.refs_4_), channel_id=1, source_target_pairs={{0,1},{1,0},{2,3},{3,2},{4,5},{5,4},{6,7},{7,6},{8,9},{9,8},{10,11... | collective-permute-start | bytes 786440 | tf_op jit(solution)/shard_map/ppermute | solution.py:135
  21.1 1.6 %copy-start.1 = (bf16[512,2048]{1,0:T(8,128)(2,1)S(1)}, bf16[512,2048]{1,0:T(8,128)(2,1)}, u32[]{:S(2)}) copy-start(bf16[512,2048]{1,0:T(8,128)(2,1)} %refs_1_.3) | copy-start | bytes 6291460
  30.4 8.0 %collective-permute-start.8 = (f32[64,2048]{1,0:T(8,128)S(1)}, f32[64,2048]{1,0:T(8,128)S(1)}, u32[]{:S(2)}, u32[]{:S(2)}) collective-permute-start(f32[64,2048]{1,0:T(8,128)S(1)} %get-tuple-element.17), channel_id=1, source_target_pairs={{0,1},{1,0},{2,3},{3,2},{4,5},{5,4},{6,7},{7,6},{8,9},{9,8},{10,11... | collective-permute-start | bytes 1572872 | tf_op jit(solution)/shard_map/ppermute | solution.py:135
  38.4 1.9 %collective-permute-start.12 = (f32[64,2048]{1,0:T(8,128)S(1)}, f32[64,2048]{1,0:T(8,128)S(1)}, u32[]{:S(2)}, u32[]{:S(2)}) collective-permute-start(f32[64,2048]{1,0:T(8,128)S(1)} %get-tuple-element.19), channel_id=1, source_target_pairs={{0,1},{1,0},{2,3},{3,2},{4,5},{5,4},{6,7},{7,6},{8,9},{9,8},{10,11... | collective-permute-start | bytes 1572872 | tf_op jit(solution)/shard_map/ppermute | solution.py:135
  38.6 8.8 %collective-permute-start.9 = (f32[32,2048]{1,0:T(8,128)S(1)}, f32[32,2048]{1,0:T(8,128)S(1)}, u32[]{:S(2)}, u32[]{:S(2)}) collective-permute-start(f32[32,2048]{1,0:T(8,128)S(1)} %slice.75), channel_id=1, source_target_pairs={{0,2},{1,3},{2,0},{3,1},{4,6},{5,7},{6,4},{7,5},{8,10},{9,11},{10,... | collective-permute-start | bytes 786440 | tf_op jit(solution)/shard_map/ppermute | solution.py:135
  40.4 8.4 %collective-permute-start.13 = (f32[32,2048]{1,0:T(8,128)S(1)}, f32[32,2048]{1,0:T(8,128)S(1)}, u32[]{:S(2)}, u32[]{:S(2)}) collective-permute-start(f32[32,2048]{1,0:T(8,128)S(1)} %slice.81), channel_id=1, source_target_pairs={{0,4},{1,5},{2,6},{3,7},{4,0},{5,1},{6,2},{7,3},{8,12},{9,13},{10,... | collective-permute-start | bytes 786440 | tf_op jit(solution)/shard_map/ppermute | solution.py:135
  47.4 5.2 %collective-permute-start.10 = (f32[16,2048]{1,0:T(8,128)S(1)}, f32[16,2048]{1,0:T(8,128)S(1)}, u32[]{:S(2)}, u32[]{:S(2)}) collective-permute-start(f32[16,2048]{1,0:T(8,128)S(1)} %slice.77), channel_id=1, source_target_pairs={{0,4},{1,5},{2,6},{3,7},{4,0},{5,1},{6,2},{7,3},{8,12},{9,13},{10,... | collective-permute-start | bytes 393224 | tf_op jit(solution)/shard_map/ppermute | solution.py:135
  48.9 6.2 %collective-permute-start.14 = (f32[16,2048]{1,0:T(8,128)S(1)}, f32[16,2048]{1,0:T(8,128)S(1)}, u32[]{:S(2)}, u32[]{:S(2)}) collective-permute-start(f32[16,2048]{1,0:T(8,128)S(1)} %slice.83), channel_id=1, source_target_pairs={{0,2},{1,3},{2,0},{3,1},{4,6},{5,7},{6,4},{7,5},{8,10},{9,11},{10,... | collective-permute-start | bytes 393224 | tf_op jit(solution)/shard_map/ppermute | solution.py:135
  52.6 7.3 %collective-permute-start.11 = (f32[8,2048]{1,0:T(8,128)S(1)}, f32[8,2048]{1,0:T(8,128)S(1)}, u32[]{:S(2)}, u32[]{:S(2)}) collective-permute-start(f32[8,2048]{1,0:T(8,128)S(1)} %slice.79), channel_id=1, source_target_pairs={{0,8},{1,9},{2,10},{3,11},{4,12},{5,13},{6,14},{7,15},{8,0},{9,1},... | collective-permute-start | bytes 196616 | tf_op jit(solution)/shard_map/ppermute | solution.py:135
  55.1 6.2 %collective-permute-start.15 = (f32[8,2048]{1,0:T(8,128)S(1)}, f32[8,2048]{1,0:T(8,128)S(1)}, u32[]{:S(2)}, u32[]{:S(2)}) collective-permute-start(f32[8,2048]{1,0:T(8,128)S(1)} %slice.85), channel_id=1, source_target_pairs={{0,8},{1,9},{2,10},{3,11},{4,12},{5,13},{6,14},{7,15},{8,0},{9,1},... | collective-permute-start | bytes 196616 | tf_op jit(solution)/shard_map/ppermute | solution.py:135

commit v4 on v1

v4 whole, which is shorter than its diff:
```python
import jax
import jax.numpy as jnp
from jax import lax
from jax.experimental import pallas as pl
from jax.experimental.pallas import tpu as pltpu
from jax.sharding import PartitionSpec as P

HEAD_DIM = 64
LANES = 128
SCALE = HEAD_DIM ** -0.5
NEG = -1e30
F32 = jnp.float32
BF16 = jnp.bfloat16

CHUNKS = ((0.5, 0), (0.5, 1))
PAIRS_PER_STEP = 4


def dot(a, b, ca, cb):
    return lax.dot_general(a, b, (((ca,), (cb,)), ((), ())), preferred_element_type=F32)


def pair_pass(q, do, k2, v2, bias, tokens, memory):
    s = dot(k2, q, 1, 1).reshape(2, memory, tokens) + bias
    e = jnp.exp(s - jnp.max(s, axis=1, keepdims=True))
    p = e * (1.0 / jnp.sum(e, axis=1, keepdims=True))
    p_low = p.astype(BF16).reshape(2 * memory, tokens)
    att = dot(v2, p_low, 0, 0).astype(BF16)
    grad_p = dot(v2, do, 1, 1).reshape(2, memory, tokens)
    delta = (do.T.astype(F32) * att.astype(F32)).reshape(2, HEAD_DIM, tokens)
    delta = jnp.sum(delta, axis=1, keepdims=True)
    grad_s = (p * (grad_p - delta)).astype(BF16).reshape(2 * memory, tokens)
    dq = dot(k2, grad_s, 0, 0).astype(BF16)
    return att.T, dq.T, dot(grad_s, q, 1, 0), dot(p_low, do, 1, 0)


def attention(queries, dout, first, second, live, order, results, offset, pairs):
    tokens, width = queries.shape
    half = first.shape[0]
    memory = 2 * half
    rows = memory // len(order)
    most = max(1, PAIRS_PER_STEP * 128 // memory)
    step = max(d for d in range(1, most + 1) if all(x % d == 0 for x in (pairs, offset)))
    block = step * LANES

    def body(*refs):
        q_ref, do_ref, ka_ref, kb_ref, va_ref, vb_ref, fa_ref, fb_ref = refs[:8]
        att_ref, dq_ref, lo_ref, hi_ref = refs[-4:]
        flags = jnp.concatenate([fa_ref[...], fb_ref[...]], axis=0).astype(F32)
        flags = jnp.concatenate([flags[at * rows : (at + 1) * rows, :1] for at in order], axis=0)
        bias = jnp.where(flags > 0, 0.0, NEG)
        left = lax.broadcasted_iota(jnp.int32, (memory, LANES), 1) < HEAD_DIM
        zero = jnp.zeros((memory, LANES), BF16)

        def both(x):
            return jnp.concatenate([jnp.where(left, x, zero), jnp.where(left, zero, x)], axis=0)

        for i in range(step):
            c = pl.ds(i * LANES, LANES)
            k = jnp.concatenate([ka_ref[:, c], kb_ref[:, c]], axis=0) * jnp.asarray(SCALE, BF16)
            v = jnp.concatenate([va_ref[:, c], vb_ref[:, c]], axis=0)
            att, dq, dk, dv = pair_pass(q_ref[:, c], do_ref[:, c], both(k), both(v), bias, tokens, memory)
            att_ref[:, c] = att
            dq_ref[:, c] = dq
            dk = jnp.where(left, dk[:memory], dk[memory:]) * SCALE
            dv = jnp.where(left, dv[:memory], dv[memory:])
            tc = pl.ds(2 * i * LANES, 2 * LANES)
            lo_ref[:, tc] = jnp.concatenate([dk[:half], dv[:half]], axis=1)
            hi_ref[:, tc] = jnp.concatenate([dk[half:], dv[half:]], axis=1)

    def cols(rows, width, start):
        return pl.BlockSpec((rows, width), lambda g: (0, g + start))

    token_spec = cols(tokens, block, offset // step)
    k_spec = cols(half, block, 0)
    v_spec = cols(half, block, pairs // step)
    flag_spec = pl.BlockSpec((half, LANES), lambda g: (0, live[0].shape[1] // LANES - 1))
    term_spec = cols(half, 2 * block, 0)
    extra = results or ()
    scratch = min(52, 12 + step * memory * tokens * 2 * 4 * 4 // 2**20)
    return pl.pallas_call(
        body,
        grid=(pairs // step,),
        in_specs=[token_spec, token_spec, k_spec, k_spec, v_spec, v_spec, flag_spec, flag_spec]
        + [pl.BlockSpec(memory_space=pl.ANY)] * len(extra),
        out_specs=[token_spec, token_spec, term_spec, term_spec],
        out_shape=[jax.ShapeDtypeStruct((tokens, width), BF16)] * 2
        + [jax.ShapeDtypeStruct((half, 2 * pairs * LANES), F32)] * 2,
        input_output_aliases={8 + i: i for i in range(len(extra))},
        compiler_params=pltpu.CompilerParams(
            dimension_semantics=("arbitrary",), vmem_limit_bytes=scratch * 2**20
        ),
        cost_estimate=pl.CostEstimate(
            flops=pairs * 12 * tokens * 2 * memory * LANES,
            transcendentals=pairs * tokens * 2 * memory,
            bytes_accessed=pairs * LANES * 8 * (tokens + 2 * memory),
        ),
    )(queries, dout, first, second, first, second, *live, *extra)


def split_pairs(total):
    chunks, done, share = [], 0, 0.0
    for part, turn in CHUNKS:
        share += part
        end = min(total, round(share * total))
        if end > done:
            chunks.append((done, end - done, turn))
        done = end
    assert done == total
    return chunks


def solution(mesh):
    n = mesh.shape["ctx"]
    bits = [1 << b for b in range(n.bit_length() - 1)]
    assert n == 1 << len(bits)

    def reduce_order(turn):
        order = list(bits)
        if turn and len(order) > 2:
            order[1], order[2] = order[2], order[1]
        return order

    def swap(x, bit):
        return lax.ppermute(x, "ctx", [(i, i ^ bit) for i in range(n)])

    def gather(chunks, orders):
        chunks = list(chunks)
        for step in range(len(bits) - 1):
            before = None
            for k, order in enumerate(orders):
                received = swap(chunks[k], order[step])
                if before is not None:
                    received, _ = lax.optimization_barrier((received, before))
                chunks[k] = before = jnp.concatenate([chunks[k], received], axis=0)
        return [(x, swap(x, order[-1])) for x, order in zip(chunks, orders)]

    def places(order):
        return [sum(b for i, b in enumerate(order) if j >> i & 1) for j in range(n)]

    def scatter(keep, send, order):
        x = keep + swap(send, order[0])
        for bit in order[1:]:
            half = x.shape[0] // 2
            x = x[:half] + swap(x[half:], bit)
        return x

    def per_device(queries, keys, values, lengths, dout):
        rows, width = keys.shape
        chunks = split_pairs(width // LANES)
        orders = [reduce_order(turn) for _, _, turn in chunks]
        live = lax.broadcasted_iota(jnp.int32, (rows, LANES), 0) < lengths[0]
        packed = []
        for start, pairs, _ in chunks:
            cols = slice(start * LANES, (start + pairs) * LANES)
            parts = [keys[:, cols], values[:, cols]] + ([] if packed else [live.astype(BF16)])
            packed.append(jnp.concatenate(parts, axis=1))
        gathered = gather(packed, [order[::-1] for order in orders])
        flag_places = places(orders[0][::-1])
        results, sums = None, []
        for (start, pairs, _), order, (first, second) in zip(chunks, orders, gathered):
            tokens = (queries, dout)
            if not start:
                tokens = [pltpu.with_memory_space_constraint(x, pltpu.MemorySpace.HBM) for x in tokens]
            at = [flag_places.index(p) for p in places(order[::-1])]
            out = attention(*tokens,  first, second, gathered[0], at, results, start, pairs)
            results = out[:2]
            sums.append(scatter(*out[2:], order))
        total = jnp.concatenate(sums, axis=1).reshape(rows, width // LANES, 2, LANES)
        key_grad = total[:, :, 0].reshape(rows, width).astype(BF16)
        value_grad = total[:, :, 1].reshape(rows, width).astype(BF16)
        return (*results, key_grad, value_grad)

    spec = P(("groups", "ctx"), None)
    return jax.shard_map(
        per_device,
        mesh=mesh,
        in_specs=(spec, spec, spec, P(("groups", "ctx")), spec),
        out_specs=(spec,) * 4,
        check_vma=False,
    )
```

time: 76.7 us -> 60.2 us (0.78)
  waiting for transfers between devices: 41 us -> 19.4 us
  starting transfers between devices: 13 us -> 20.9 us
  other arithmetic: 3.43 us -> 0.32 us
  Pallas kernels: 15.2 us -> 16.2 us
  local copies, waits for them, and re-layouts: 2.36 us -> 1.57 us
    ppermute x8 -> x16, waiting for transfers between devices: 41 us -> 19.4 us  [swap(): return lax.ppermute(x, 'ctx', [(i, i ^ bit) for i in range(n)])]
    ppermute x8 -> x16, starting transfers between devices: 13 us -> 20.9 us  [swap(): return lax.ppermute(x, 'ctx', [(i, i ^ bit) for i in range(n)])]
    concatenate x4 -> x8, other arithmetic: 3.19 us -> 0.09 us  [the longest x6 0.07 us: gather(): chunks[k] = before = jnp.concatenate([chunks[k], received], axis=0)]
    unnamed x2 -> x4, local copies, waits for them, and re-layouts: 1.59 us -> 0.01 us
    pallas_call x1 -> x2, Pallas kernels: 15.2 us -> 16.2 us  [attention(): pl.pallas_call(body, grid=(pairs // step,), in_specs=[token_spec, token_s...]
    slice x0 -> x1, local copies, waits for them, and re-layouts: none -> 0.78 us  [per_device(): keys[:, cols]]
  transfers between devices with their start and end apart: 8 -> 16, of which waited for: 8 -> 12; matrix products, arithmetic and copies ran while one was open for 0% -> 1% of each run, Pallas kernels for 0% -> 27%
where the time goes in v4:
time: 60.2 us; the launch traced here: 59.9 us
  starting transfers between devices  20.9 us (35%)
  waiting for transfers between devices  19.4 us (32%)
  Pallas kernels  16.2 us (27%)
  local copies, waits for them, and re-layouts  1.57 us (3%)
  between operations  1.44 us (2%)
    ppermute x16, starting transfers between devices, swap(): return lax.ppermute(x, 'ctx', [(i, i ^ bit) for i in range(n)])  20.9 us
    ppermute x16, waiting for transfers between devices, swap(): return lax.ppermute(x, 'ctx', [(i, i ^ bit) for i in range(n)])  19.4 us
    pallas_call x2, Pallas kernels, attention(): pl.pallas_call(body, grid=(pairs // step,), in_specs=[token_spec, token_s...  16.2 us
  transfers between devices with their start and end apart: 16, of which 12 were waited for; matrix products, arithmetic and copies ran while one was open for 1% of the time, Pallas kernels for 27%

profile of v4, /device:TPU:0, one launch (start us, length us, event | category | flops | bytes accessed | tf_op | source)
XLA Modules:
  0.0 59.9 jit_solution(6616417879958101853)
XLA Ops:
  1.3 0.8 %fusion = (bf16[8,1024]{1,0:T(8,128)(2,1)S(1)}, bf16[8,1024]{1,0:T(8,128)(2,1)S(1)}, bf16[8,1024]{1,0:T(8,128)(2,1)S(1)}, bf16[8,1024]{1,0:T(8,128)(2,1)S(1)}) fusion(bf16[8,2048]{1,0:T(8,128)(2,1)} %param.6, bf16[8,2048]{1,0:T(8,128)(2,1)} %param.7), kind=kLoop, calls=%fused_computation.18 | loop fusion | bytes 131072 | tf_op jit(solution)/shard_map/slice | solution.py:156
  2.1 0.1 iota.7
  2.1 4.0 %collective-permute-start.1 = (bf16[8,2176]{1,0:T(8,128)(2,1)S(1)}, bf16[8,2176]{1,0:T(8,128)(2,1)S(1)}, u32[]{:S(2)}, u32[]{:S(2)}) collective-permute-start(bf16[8,2176]{1,0:T(8,128)(2,1)S(1)} %pad_maximum_fusion.6), channel_id=1, source_target_pairs={{0,8},{1,9},{2,10},{3,11},{4,12},{5,13},{6,14},{7,15},{8,0},{9,1},... | collective-permute-start | bytes 104456 | tf_op jit(solution)/shard_map/ppermute | solution.py:125
  6.2 0.1 collective-permute-start
  6.3 2.2 %collective-permute-done.1 = bf16[8,2176]{1,0:T(8,128)(2,1)S(1)} collective-permute-done((bf16[8,2176]{1,0:T(8,128)(2,1)S(1)}, bf16[8,2176]{1,0:T(8,128)(2,1)S(1)}, u32[]{:S(2)}, u32[]{:S(2)}) %collective-permute-start.1) | collective-permute-done | bytes 34848 | tf_op jit(solution)/shard_map/ppermute | solution.py:125
  8.5 1.7 %collective-permute-start.3 = (bf16[16,2176]{1,0:T(8,128)(2,1)S(1)}, bf16[16,2176]{1,0:T(8,128)(2,1)S(1)}, u32[]{:S(2)}, u32[]{:S(2)}) collective-permute-start(bf16[16,2176]{1,0:T(8,128)(2,1)S(1)} %pad_maximum_fusion.4), channel_id=1, source_target_pairs={{0,4},{1,5},{2,6},{3,7},{4,0},{5,1},{6,2},{7,3},{8,12},{9,13},{10,... | collective-permute-start | bytes 208904 | tf_op jit(solution)/shard_map/ppermute | solution.py:125
  10.2 0.8 %collective-permute-done = bf16[8,2048]{1,0:T(8,128)(2,1)S(1)} collective-permute-done((bf16[8,2048]{1,0:T(8,128)(2,1)S(1)}, bf16[8,2048]{1,0:T(8,128)(2,1)S(1)}, u32[]{:S(2)}, u32[]{:S(2)}) %collective-permute-start) | collective-permute-done | bytes 32800 | tf_op jit(solution)/shard_map/ppermute | solution.py:125
  11.0 1.5 %collective-permute-start.2 = (bf16[16,2048]{1,0:T(8,128)(2,1)S(1)}, bf16[16,2048]{1,0:T(8,128)(2,1)S(1)}, u32[]{:S(2)}, u32[]{:S(2)}) collective-permute-start(bf16[16,2048]{1,0:T(8,128)(2,1)S(1)} %pad_maximum_fusion.5), channel_id=1, source_target_pairs={{0,2},{1,3},{2,0},{3,1},{4,6},{5,7},{6,4},{7,5},{8,10},{9,11},{10,... | collective-permute-start | bytes 196616 | tf_op jit(solution)/shard_map/ppermute | solution.py:125
  12.5 0.3 collective-permute-done.3
  12.8 1.8 %collective-permute-start.5 = (bf16[32,2176]{1,0:T(8,128)(2,1)S(1)}, bf16[32,2176]{1,0:T(8,128)(2,1)S(1)}, u32[]{:S(2)}, u32[]{:S(2)}) collective-permute-start(bf16[32,2176]{1,0:T(8,128)(2,1)S(1)} %pad_maximum_fusion.2), channel_id=1, source_target_pairs={{0,2},{1,3},{2,0},{3,1},{4,6},{5,7},{6,4},{7,5},{8,10},{9,11},{10,... | collective-permute-start | bytes 417800 | tf_op jit(solution)/shard_map/ppermute | solution.py:125
  14.6 1.1 %collective-permute-done.2 = bf16[16,2048]{1,0:T(8,128)(2,1)S(1)} collective-permute-done((bf16[16,2048]{1,0:T(8,128)(2,1)S(1)}, bf16[16,2048]{1,0:T(8,128)(2,1)S(1)}, u32[]{:S(2)}, u32[]{:S(2)}) %collective-permute-start.2) | collective-permute-done | bytes 65568 | tf_op jit(solution)/shard_map/ppermute | solution.py:125
  15.8 1.5 %collective-permute-start.4 = (bf16[32,2048]{1,0:T(8,128)(2,1)S(1)}, bf16[32,2048]{1,0:T(8,128)(2,1)S(1)}, u32[]{:S(2)}, u32[]{:S(2)}) collective-permute-start(bf16[32,2048]{1,0:T(8,128)(2,1)S(1)} %pad_maximum_fusion.3), channel_id=1, source_target_pairs={{0,4},{1,5},{2,6},{3,7},{4,0},{5,1},{6,2},{7,3},{8,12},{9,13},{10,... | collective-permute-start | bytes 393224 | tf_op jit(solution)/shard_map/ppermute | solution.py:125
  17.2 0.7 %collective-permute-done.5 = bf16[32,2176]{1,0:T(8,128)(2,1)S(1)} collective-permute-done((bf16[32,2176]{1,0:T(8,128)(2,1)S(1)}, bf16[32,2176]{1,0:T(8,128)(2,1)S(1)}, u32[]{:S(2)}, u32[]{:S(2)}) %collective-permute-start.5) | collective-permute-done | bytes 139296 | tf_op jit(solution)/shard_map/ppermute | solution.py:125
  18.0 0.1 collective-permute-start.7
  18.0 2.8 %collective-permute-done.4 = bf16[32,2048]{1,0:T(8,128)(2,1)S(1)} collective-permute-done((bf16[32,2048]{1,0:T(8,128)(2,1)S(1)}, bf16[32,2048]{1,0:T(8,128)(2,1)S(1)}, u32[]{:S(2)}, u32[]{:S(2)}) %collective-permute-start.4) | collective-permute-done | bytes 131104 | tf_op jit(solution)/shard_map/ppermute | solution.py:125
  20.8 0.0 copy-start
  20.8 0.0 copy-start.1
  20.8 0.1 collective-permute-start.6
  20.9 0.0 collective-permute-done.7.refs_3_.refs_5_.refs_7_
  20.9 8.7 %shard_map.84 = (bf16[512,2048]{1,0:T(8,128)(2,1)}, bf16[512,2048]{1,0:T(8,128)(2,1)}, f32[64,2048]{1,0:T(8,128)S(1)}, f32[64,2048]{1,0:T(8,128)S(1)}) custom-call(bf16[512,2048]{1,0:T(8,128)(2,1)} %refs_0_.3, bf16[512,2048]{1,0:T(8,128)(2,1)} %refs_1_.3, bf16[64,2176]{1,0:T(8,128)(2,1)S(1)} %pad_maximum_fusion.refs_2_.refs_4_.refs_6_, ...), custom_call_target="tpu_custom_call" | custom-call | flops 1610612736 | bytes 6291456 | tf_op jit(solution)/shard_map/pallas_call | solution.py:81
  29.6 0.3 collective-permute-start.8
  29.9 0.0 collective-permute-done.6.refs_3_.refs_5_
  29.9 0.0 copy-done
  29.9 0.0 copy-done.1
  29.9 7.5 %shard_map.85 = (bf16[512,2048]{1,0:T(8,128)(2,1)}, bf16[512,2048]{1,0:T(8,128)(2,1)}, f32[64,2048]{1,0:T(8,128)S(1)}, f32[64,2048]{1,0:T(8,128)S(1)}) custom-call(bf16[512,2048]{1,0:T(8,128)(2,1)S(1)} %copy-done, bf16[512,2048]{1,0:T(8,128)(2,1)S(1)} %copy-done.1, ...), custom_call_target="tpu_custom_call", output_to_operand_aliasing={{0}: (8, {}), {1}: (9, {})} | custom-call | flops 1610612736 | bytes 6291456 | tf_op jit(solution)/shard_map/pallas_call | solution.py:81
  37.4 0.2 collective-permute-start.12
  37.6 0.0 collective-permute-done.8
  37.7 0.1 add.24
  37.7 1.1 %collective-permute-start.9 = (f32[32,2048]{1,0:T(8,128)S(1)}, f32[32,2048]{1,0:T(8,128)S(1)}, u32[]{:S(2)}, u32[]{:S(2)}) collective-permute-start(f32[32,2048]{1,0:T(8,128)S(1)} %slice.75), channel_id=1, source_target_pairs={{0,2},{1,3},{2,0},{3,1},{4,6},{5,7},{6,4},{7,5},{8,10},{9,11},{10,... | collective-permute-start | bytes 786440 | tf_op jit(solution)/shard_map/ppermute | solution.py:125
  38.9 0.5 collective-permute-done.12
  39.3 0.1 add.28
  39.4 1.5 %collective-permute-start.13 = (f32[32,2048]{1,0:T(8,128)S(1)}, f32[32,2048]{1,0:T(8,128)S(1)}, u32[]{:S(2)}, u32[]{:S(2)}) collective-permute-start(f32[32,2048]{1,0:T(8,128)S(1)} %slice.81), channel_id=1, source_target_pairs={{0,4},{1,5},{2,6},{3,7},{4,0},{5,1},{6,2},{7,3},{8,12},{9,13},{10,... | collective-permute-start | bytes 786440 | tf_op jit(solution)/shard_map/ppermute | solution.py:125
  40.9 5.4 %collective-permute-done.9 = f32[32,2048]{1,0:T(8,128)S(1)} collective-permute-done((f32[32,2048]{1,0:T(8,128)S(1)}, f32[32,2048]{1,0:T(8,128)S(1)}, u32[]{:S(2)}, u32[]{:S(2)}) %collective-permute-start.9) | collective-permute-done | bytes 262176 | tf_op jit(solution)/shard_map/ppermute | solution.py:125
  46.4 1.5 %collective-permute-start.10 = (f32[16,2048]{1,0:T(8,128)S(1)}, f32[16,2048]{1,0:T(8,128)S(1)}, u32[]{:S(2)}, u32[]{:S(2)}) collective-permute-start(f32[16,2048]{1,0:T(8,128)S(1)} %slice.77), channel_id=1, source_target_pairs={{0,4},{1,5},{2,6},{3,7},{4,0},{5,1},{6,2},{7,3},{8,12},{9,13},{10,... | collective-permute-start | bytes 393224 | tf_op jit(solution)/shard_map/ppermute | solution.py:125
  47.8 0.1 collective-permute-done.13
  48.0 1.5 %collective-permute-start.14 = (f32[16,2048]{1,0:T(8,128)S(1)}, f32[16,2048]{1,0:T(8,128)S(1)}, u32[]{:S(2)}, u32[]{:S(2)}) collective-permute-start(f32[16,2048]{1,0:T(8,128)S(1)} %slice.83), channel_id=1, source_target_pairs={{0,2},{1,3},{2,0},{3,1},{4,6},{5,7},{6,4},{7,5},{8,10},{9,11},{10,... | collective-permute-start | bytes 393224 | tf_op jit(solution)/shard_map/ppermute | solution.py:125
  49.5 1.9 %collective-permute-done.10 = f32[16,2048]{1,0:T(8,128)S(1)} collective-permute-done((f32[16,2048]{1,0:T(8,128)S(1)}, f32[16,2048]{1,0:T(8,128)S(1)}, u32[]{:S(2)}, u32[]{:S(2)}) %collective-permute-start.10) | collective-permute-done | bytes 131104 | tf_op jit(solution)/shard_map/ppermute | solution.py:125
  51.4 2.5 %collective-permute-start.11 = (f32[8,2048]{1,0:T(8,128)S(1)}, f32[8,2048]{1,0:T(8,128)S(1)}, u32[]{:S(2)}, u32[]{:S(2)}) collective-permute-start(f32[8,2048]{1,0:T(8,128)S(1)} %slice.79), channel_id=1, source_target_pairs={{0,8},{1,9},{2,10},{3,11},{4,12},{5,13},{6,14},{7,15},{8,0},{9,1},... | collective-permute-start | bytes 196616 | tf_op jit(solution)/shard_map/ppermute | solution.py:125
  53.9 0.0 collective-permute-done.14
  54.0 1.6 %collective-permute-start.15 = (f32[8,2048]{1,0:T(8,128)S(1)}, f32[8,2048]{1,0:T(8,128)S(1)}, u32[]{:S(2)}, u32[]{:S(2)}) collective-permute-start(f32[8,2048]{1,0:T(8,128)S(1)} %slice.85), channel_id=1, source_target_pairs={{0,8},{1,9},{2,10},{3,11},{4,12},{5,13},{6,14},{7,15},{8,0},{9,1},... | collective-permute-start | bytes 196616 | tf_op jit(solution)/shard_map/ppermute | solution.py:125
  55.5 2.8 %collective-permute-done.11 = f32[8,2048]{1,0:T(8,128)S(1)} collective-permute-done((f32[8,2048]{1,0:T(8,128)S(1)}, f32[8,2048]{1,0:T(8,128)S(1)}, u32[]{:S(2)}, u32[]{:S(2)}) %collective-permute-start.11) | collective-permute-done | bytes 65568 | tf_op jit(solution)/shard_map/ppermute | solution.py:125
  58.4 0.8 %collective-permute-done.15 = f32[8,2048]{1,0:T(8,128)S(1)} collective-permute-done((f32[8,2048]{1,0:T(8,128)S(1)}, f32[8,2048]{1,0:T(8,128)S(1)}, u32[]{:S(2)}, u32[]{:S(2)}) %collective-permute-start.15) | collective-permute-done | bytes 65568 | tf_op jit(solution)/shard_map/ppermute | solution.py:125
  59.2 0.6 %slice_bitcast_fusion = (bf16[8,2048]{1,0:T(8,128)(2,1)}, bf16[8,2048]{1,0:T(8,128)(2,1)}) fusion(bf16[8,16,2,128]{3,0,2,1:T(8,128)(2,1)S(1)} %bitcast.7), kind=kLoop, calls=%fused_computation.14 | loop fusion | bytes 131072 | tf_op jit(solution)/shard_map/convert_element_type | solution.py:171
  (22 shorter events, 0.3 us)
Async XLA Ops:
  2.1 6.3 %collective-permute-start.1 = (bf16[8,2176]{1,0:T(8,128)(2,1)S(1)}, bf16[8,2176]{1,0:T(8,128)(2,1)S(1)}, u32[]{:S(2)}, u32[]{:S(2)}) collective-permute-start(bf16[8,2176]{1,0:T(8,128)(2,1)S(1)} %pad_maximum_fusion.6), channel_id=1, source_target_pairs={{0,8},{1,9},{2,10},{3,11},{4,12},{5,13},{6,14},{7,15},{8,0},{9,1},... | collective-permute-start | bytes 104456 | tf_op jit(solution)/shard_map/ppermute | solution.py:125
  6.2 4.8 %collective-permute-start = (bf16[8,2048]{1,0:T(8,128)(2,1)S(1)}, bf16[8,2048]{1,0:T(8,128)(2,1)S(1)}, u32[]{:S(2)}, u32[]{:S(2)}) collective-permute-start(bf16[8,2048]{1,0:T(8,128)(2,1)S(1)} %pad_maximum_fusion.7), channel_id=1, source_target_pairs={{0,8},{1,9},{2,10},{3,11},{4,12},{5,13},{6,14},{7,15},{8,0},{9,1},... | collective-permute-start | bytes 98312 | tf_op jit(solution)/shard_map/ppermute | solution.py:125
  8.5 4.3 %collective-permute-start.3 = (bf16[16,2176]{1,0:T(8,128)(2,1)S(1)}, bf16[16,2176]{1,0:T(8,128)(2,1)S(1)}, u32[]{:S(2)}, u32[]{:S(2)}) collective-permute-start(bf16[16,2176]{1,0:T(8,128)(2,1)S(1)} %pad_maximum_fusion.4), channel_id=1, source_target_pairs={{0,4},{1,5},{2,6},{3,7},{4,0},{5,1},{6,2},{7,3},{8,12},{9,13},{10,... | collective-permute-start | bytes 208904 | tf_op jit(solution)/shard_map/ppermute | solution.py:125
  11.0 4.7 %collective-permute-start.2 = (bf16[16,2048]{1,0:T(8,128)(2,1)S(1)}, bf16[16,2048]{1,0:T(8,128)(2,1)S(1)}, u32[]{:S(2)}, u32[]{:S(2)}) collective-permute-start(bf16[16,2048]{1,0:T(8,128)(2,1)S(1)} %pad_maximum_fusion.5), channel_id=1, source_target_pairs={{0,2},{1,3},{2,0},{3,1},{4,6},{5,7},{6,4},{7,5},{8,10},{9,11},{10,... | collective-permute-start | bytes 196616 | tf_op jit(solution)/shard_map/ppermute | solution.py:125
  12.8 5.1 %collective-permute-start.5 = (bf16[32,2176]{1,0:T(8,128)(2,1)S(1)}, bf16[32,2176]{1,0:T(8,128)(2,1)S(1)}, u32[]{:S(2)}, u32[]{:S(2)}) collective-permute-start(bf16[32,2176]{1,0:T(8,128)(2,1)S(1)} %pad_maximum_fusion.2), channel_id=1, source_target_pairs={{0,2},{1,3},{2,0},{3,1},{4,6},{5,7},{6,4},{7,5},{8,10},{9,11},{10,... | collective-permute-start | bytes 417800 | tf_op jit(solution)/shard_map/ppermute | solution.py:125
  15.8 5.0 %collective-permute-start.4 = (bf16[32,2048]{1,0:T(8,128)(2,1)S(1)}, bf16[32,2048]{1,0:T(8,128)(2,1)S(1)}, u32[]{:S(2)}, u32[]{:S(2)}) collective-permute-start(bf16[32,2048]{1,0:T(8,128)(2,1)S(1)} %pad_maximum_fusion.3), channel_id=1, source_target_pairs={{0,4},{1,5},{2,6},{3,7},{4,0},{5,1},{6,2},{7,3},{8,12},{9,13},{10,... | collective-permute-start | bytes 393224 | tf_op jit(solution)/shard_map/ppermute | solution.py:125
  18.0 3.0 %collective-permute-start.7 = (bf16[64,2176]{1,0:T(8,128)(2,1)S(1)}, bf16[64,2176]{1,0:T(8,128)(2,1)S(1)}, u32[]{:S(2)}, u32[]{:S(2)}) collective-permute-start(bf16[64,2176]{1,0:T(8,128)(2,1)S(1)} %pad_maximum_fusion.refs_2_.refs_4_.refs_6_), channel_id=1, source_target_pairs={{0,1},{1,0},{2,3},{3,2},{4,5},{5,4},{6,7},{7,6},{8,9},{9,8},{10,11... | collective-permute-start | bytes 835592 | tf_op jit(solution)/shard_map/ppermute | solution.py:125
  20.8 9.1 %copy-start = (bf16[512,2048]{1,0:T(8,128)(2,1)S(1)}, bf16[512,2048]{1,0:T(8,128)(2,1)}, u32[]{:S(2)}) copy-start(bf16[512,2048]{1,0:T(8,128)(2,1)} %refs_0_.3) | copy-start | bytes 6291460
  20.8 9.1 %copy-start.1 = (bf16[512,2048]{1,0:T(8,128)(2,1)S(1)}, bf16[512,2048]{1,0:T(8,128)(2,1)}, u32[]{:S(2)}) copy-start(bf16[512,2048]{1,0:T(8,128)(2,1)} %refs_1_.3) | copy-start | bytes 6291460
  20.8 9.0 %collective-permute-start.6 = (bf16[64,2048]{1,0:T(8,128)(2,1)S(1)}, bf16[64,2048]{1,0:T(8,128)(2,1)S(1)}, u32[]{:S(2)}, u32[]{:S(2)}) collective-permute-start(bf16[64,2048]{1,0:T(8,128)(2,1)S(1)} %pad_maximum_fusion.1.refs_2_.refs_4_), channel_id=1, source_target_pairs={{0,1},{1,0},{2,3},{3,2},{4,5},{5,4},{6,7},{7,6},{8,9},{9,8},{10,11... | collective-permute-start | bytes 786440 | tf_op jit(solution)/shard_map/ppermute | solution.py:125
  29.6 8.1 %collective-permute-start.8 = (f32[64,2048]{1,0:T(8,128)S(1)}, f32[64,2048]{1,0:T(8,128)S(1)}, u32[]{:S(2)}, u32[]{:S(2)}) collective-permute-start(f32[64,2048]{1,0:T(8,128)S(1)} %get-tuple-element.23), channel_id=1, source_target_pairs={{0,1},{1,0},{2,3},{3,2},{4,5},{5,4},{6,7},{7,6},{8,9},{9,8},{10,11... | collective-permute-start | bytes 1572872 | tf_op jit(solution)/shard_map/ppermute | solution.py:125
  37.4 1.9 %collective-permute-start.12 = (f32[64,2048]{1,0:T(8,128)S(1)}, f32[64,2048]{1,0:T(8,128)S(1)}, u32[]{:S(2)}, u32[]{:S(2)}) collective-permute-start(f32[64,2048]{1,0:T(8,128)S(1)} %get-tuple-element.25), channel_id=1, source_target_pairs={{0,1},{1,0},{2,3},{3,2},{4,5},{5,4},{6,7},{7,6},{8,9},{9,8},{10,11... | collective-permute-start | bytes 1572872 | tf_op jit(solution)/shard_map/ppermute | solution.py:125
  37.7 8.6 %collective-permute-start.9 = (f32[32,2048]{1,0:T(8,128)S(1)}, f32[32,2048]{1,0:T(8,128)S(1)}, u32[]{:S(2)}, u32[]{:S(2)}) collective-permute-start(f32[32,2048]{1,0:T(8,128)S(1)} %slice.75), channel_id=1, source_target_pairs={{0,2},{1,3},{2,0},{3,1},{4,6},{5,7},{6,4},{7,5},{8,10},{9,11},{10,... | collective-permute-start | bytes 786440 | tf_op jit(solution)/shard_map/ppermute | solution.py:125
  39.4 8.5 %collective-permute-start.13 = (f32[32,2048]{1,0:T(8,128)S(1)}, f32[32,2048]{1,0:T(8,128)S(1)}, u32[]{:S(2)}, u32[]{:S(2)}) collective-permute-start(f32[32,2048]{1,0:T(8,128)S(1)} %slice.81), channel_id=1, source_target_pairs={{0,4},{1,5},{2,6},{3,7},{4,0},{5,1},{6,2},{7,3},{8,12},{9,13},{10,... | collective-permute-start | bytes 786440 | tf_op jit(solution)/shard_map/ppermute | solution.py:125
  46.4 5.0 %collective-permute-start.10 = (f32[16,2048]{1,0:T(8,128)S(1)}, f32[16,2048]{1,0:T(8,128)S(1)}, u32[]{:S(2)}, u32[]{:S(2)}) collective-permute-start(f32[16,2048]{1,0:T(8,128)S(1)} %slice.77), channel_id=1, source_target_pairs={{0,4},{1,5},{2,6},{3,7},{4,0},{5,1},{6,2},{7,3},{8,12},{9,13},{10,... | collective-permute-start | bytes 393224 | tf_op jit(solution)/shard_map/ppermute | solution.py:125
  48.0 6.0 %collective-permute-start.14 = (f32[16,2048]{1,0:T(8,128)S(1)}, f32[16,2048]{1,0:T(8,128)S(1)}, u32[]{:S(2)}, u32[]{:S(2)}) collective-permute-start(f32[16,2048]{1,0:T(8,128)S(1)} %slice.83), channel_id=1, source_target_pairs={{0,2},{1,3},{2,0},{3,1},{4,6},{5,7},{6,4},{7,5},{8,10},{9,11},{10,... | collective-permute-start | bytes 393224 | tf_op jit(solution)/shard_map/ppermute | solution.py:125
  51.4 7.0 %collective-permute-start.11 = (f32[8,2048]{1,0:T(8,128)S(1)}, f32[8,2048]{1,0:T(8,128)S(1)}, u32[]{:S(2)}, u32[]{:S(2)}) collective-permute-start(f32[8,2048]{1,0:T(8,128)S(1)} %slice.79), channel_id=1, source_target_pairs={{0,8},{1,9},{2,10},{3,11},{4,12},{5,13},{6,14},{7,15},{8,0},{9,1},... | collective-permute-start | bytes 196616 | tf_op jit(solution)/shard_map/ppermute | solution.py:125
  54.0 5.2 %collective-permute-start.15 = (f32[8,2048]{1,0:T(8,128)S(1)}, f32[8,2048]{1,0:T(8,128)S(1)}, u32[]{:S(2)}, u32[]{:S(2)}) collective-permute-start(f32[8,2048]{1,0:T(8,128)S(1)} %slice.85), channel_id=1, source_target_pairs={{0,8},{1,9},{2,10},{3,11},{4,12},{5,13},{6,14},{7,15},{8,0},{9,1},... | collective-permute-start | bytes 196616 | tf_op jit(solution)/shard_map/ppermute | solution.py:125

commit v5 on v4

--- a/solution.py
+++ b/solution.py
@@ -18,20 +18,6 @@
 
 def dot(a, b, ca, cb):
     return lax.dot_general(a, b, (((ca,), (cb,)), ((), ())), preferred_element_type=F32)
-
-
-def pair_pass(q, do, k2, v2, bias, tokens, memory):
-    s = dot(k2, q, 1, 1).reshape(2, memory, tokens) + bias
-    e = jnp.exp(s - jnp.max(s, axis=1, keepdims=True))
-    p = e * (1.0 / jnp.sum(e, axis=1, keepdims=True))
-    p_low = p.astype(BF16).reshape(2 * memory, tokens)
-    att = dot(v2, p_low, 0, 0).astype(BF16)
-    grad_p = dot(v2, do, 1, 1).reshape(2, memory, tokens)
-    delta = (do.T.astype(F32) * att.astype(F32)).reshape(2, HEAD_DIM, tokens)
-    delta = jnp.sum(delta, axis=1, keepdims=True)
-    grad_s = (p * (grad_p - delta)).astype(BF16).reshape(2 * memory, tokens)
-    dq = dot(k2, grad_s, 0, 0).astype(BF16)
-    return att.T, dq.T, dot(grad_s, q, 1, 0), dot(p_low, do, 1, 0)
 
 
 def attention(queries, dout, first, second, live, order, results, offset, pairs):
@@ -55,27 +41,59 @@
         def both(x):
             return jnp.concatenate([jnp.where(left, x, zero), jnp.where(left, zero, x)], axis=0)
 
-        for i in range(step):
-            c = pl.ds(i * LANES, LANES)
-            k = jnp.concatenate([ka_ref[:, c], kb_ref[:, c]], axis=0) * jnp.asarray(SCALE, BF16)
-            v = jnp.concatenate([va_ref[:, c], vb_ref[:, c]], axis=0)
-            att, dq, dk, dv = pair_pass(q_ref[:, c], do_ref[:, c], both(k), both(v), bias, tokens, memory)
-            att_ref[:, c] = att
-            dq_ref[:, c] = dq
-            dk = jnp.where(left, dk[:memory], dk[memory:]) * SCALE
-            dv = jnp.where(left, dv[:memory], dv[memory:])
-            tc = pl.ds(2 * i * LANES, 2 * LANES)
-            lo_ref[:, tc] = jnp.concatenate([dk[:half], dv[:half]], axis=1)
-            hi_ref[:, tc] = jnp.concatenate([dk[half:], dv[half:]], axis=1)
+        pair = [{} for _ in range(step)]
+        cols = [pl.ds(i * LANES, LANES) for i in range(step)]
 
-    def cols(rows, width, start):
+        def scores(i):
+            k = jnp.concatenate([ka_ref[:, cols[i]], kb_ref[:, cols[i]]], axis=0) * jnp.asarray(SCALE, BF16)
+            v = jnp.concatenate([va_ref[:, cols[i]], vb_ref[:, cols[i]]], axis=0)
+            pair[i].update(k=both(k), v=both(v))
+            pair[i]["s"] = dot(pair[i]["k"], q_ref[:, cols[i]], 1, 1).reshape(2, memory, tokens) + bias
+            pair[i]["grad_p"] = dot(pair[i]["v"], do_ref[:, cols[i]], 1, 1).reshape(2, memory, tokens)
+
+        def softmax(i):
+            s = pair[i].pop("s")
+            e = jnp.exp(s - jnp.max(s, axis=1, keepdims=True))
+            pair[i]["p"] = e * (1.0 / jnp.sum(e, axis=1, keepdims=True))
+            pair[i]["p_low"] = pair[i]["p"].astype(BF16).reshape(2 * memory, tokens)
+
+        def attended(i):
+            pair[i]["att"] = dot(pair[i]["v"], pair[i]["p_low"], 0, 0).astype(BF16)
+            dv = dot(pair[i].pop("p_low"), do_ref[:, cols[i]], 1, 0)
+            store(2 * i + 1, jnp.where(left, dv[:memory], dv[memory:]))
+
+        def score_grads(i):
+            att = pair[i].pop("att")
+            delta = (do_ref[:, cols[i]].T.astype(F32) * att.astype(F32)).reshape(2, HEAD_DIM, tokens)
+            delta = jnp.sum(delta, axis=1, keepdims=True)
+            grad_s = pair[i].pop("p") * (pair[i].pop("grad_p") - delta)
+            pair[i]["grad_s"] = grad_s.astype(BF16).reshape(2 * memory, tokens)
+            att_ref[:, cols[i]] = att.T
+
+        def grads(i):
+            dq_ref[:, cols[i]] = dot(pair[i]["k"], pair[i]["grad_s"], 0, 0).astype(BF16).T
+            dk = dot(pair[i]["grad_s"], q_ref[:, cols[i]], 1, 0)
+            store(2 * i, jnp.where(left, dk[:memory], dk[memory:]) * SCALE)
+
+        def store(j, x):
+            c = pl.ds(j * LANES, LANES)
+            lo_ref[:, c] = x[:half]
+            hi_ref[:, c] = x[half:]
+
+        stages = (scores, softmax, attended, score_grads, grads)
+        for t in range(step + len(stages) - 1):
+            for j, stage in enumerate(stages):
+                if 0 <= t - j < step:
+                    stage(t - j)
+
+    def columns(rows, width, start):
         return pl.BlockSpec((rows, width), lambda g: (0, g + start))
 
-    token_spec = cols(tokens, block, offset // step)
-    k_spec = cols(half, block, 0)
-    v_spec = cols(half, block, pairs // step)
+    token_spec = columns(tokens, block, offset // step)
+    k_spec = columns(half, block, 0)
+    v_spec = columns(half, block, pairs // step)
     flag_spec = pl.BlockSpec((half, LANES), lambda g: (0, live[0].shape[1] // LANES - 1))
-    term_spec = cols(half, 2 * block, 0)
+    term_spec = columns(half, 2 * block, 0)
     extra = results or ()
     scratch = min(52, 12 + step * memory * tokens * 2 * 4 * 4 // 2**20)
     return pl.pallas_call(

time: 60.2 us -> 54.7 us (0.909)
  Pallas kernels: 16.2 us -> 10.7 us
    pallas_call x2, Pallas kernels: 16.2 us -> 10.7 us  [attention(): pl.pallas_call(body, grid=(pairs // step,), in_specs=[token_spec, token_s...]
  transfers between devices with their start and end apart: 16 -> 16, of which waited for: 12 -> 12; matrix products, arithmetic and copies ran while one was open for 1% -> 1% of each run, Pallas kernels for 27% -> 20%
where the time goes in v5:
time: 54.7 us; the launch traced here: 54.4 us
  starting transfers between devices  20.8 us (38%)
  waiting for transfers between devices  19.5 us (36%)
  Pallas kernels  10.7 us (20%)
  local copies, waits for them, and re-layouts  1.57 us (3%)
  between operations  1.44 us (3%)
    ppermute x16, starting transfers between devices, swap(): return lax.ppermute(x, 'ctx', [(i, i ^ bit) for i in range(n)])  20.8 us
    ppermute x16, waiting for transfers between devices, swap(): return lax.ppermute(x, 'ctx', [(i, i ^ bit) for i in range(n)])  19.5 us
    pallas_call x2, Pallas kernels, attention(): pl.pallas_call(body, grid=(pairs // step,), in_specs=[token_spec, token_s...  10.7 us
  transfers between devices with their start and end apart: 16, of which 12 were waited for; matrix products, arithmetic and copies ran while one was open for 1% of the time, Pallas kernels for 20%

profile of v5, /device:TPU:0, one launch (start us, length us, event | category | flops | bytes accessed | tf_op | source)
XLA Modules:
  0.0 54.4 jit_solution(4699577636292403535)
XLA Ops:
  1.3 0.8 %fusion = (bf16[8,1024]{1,0:T(8,128)(2,1)S(1)}, bf16[8,1024]{1,0:T(8,128)(2,1)S(1)}, bf16[8,1024]{1,0:T(8,128)(2,1)S(1)}, bf16[8,1024]{1,0:T(8,128)(2,1)S(1)}) fusion(bf16[8,2048]{1,0:T(8,128)(2,1)} %param.6, bf16[8,2048]{1,0:T(8,128)(2,1)} %param.7), kind=kLoop, calls=%fused_computation.18 | loop fusion | bytes 131072 | tf_op jit(solution)/shard_map/slice | solution.py:174
  2.1 0.1 iota.7
  2.1 4.0 %collective-permute-start.1 = (bf16[8,2176]{1,0:T(8,128)(2,1)S(1)}, bf16[8,2176]{1,0:T(8,128)(2,1)S(1)}, u32[]{:S(2)}, u32[]{:S(2)}) collective-permute-start(bf16[8,2176]{1,0:T(8,128)(2,1)S(1)} %pad_maximum_fusion.6), channel_id=1, source_target_pairs={{0,8},{1,9},{2,10},{3,11},{4,12},{5,13},{6,14},{7,15},{8,0},{9,1},... | collective-permute-start | bytes 104456 | tf_op jit(solution)/shard_map/ppermute | solution.py:143
  6.2 0.1 collective-permute-start
  6.3 2.2 %collective-permute-done.1 = bf16[8,2176]{1,0:T(8,128)(2,1)S(1)} collective-permute-done((bf16[8,2176]{1,0:T(8,128)(2,1)S(1)}, bf16[8,2176]{1,0:T(8,128)(2,1)S(1)}, u32[]{:S(2)}, u32[]{:S(2)}) %collective-permute-start.1) | collective-permute-done | bytes 34848 | tf_op jit(solution)/shard_map/ppermute | solution.py:143
  8.5 1.7 %collective-permute-start.3 = (bf16[16,2176]{1,0:T(8,128)(2,1)S(1)}, bf16[16,2176]{1,0:T(8,128)(2,1)S(1)}, u32[]{:S(2)}, u32[]{:S(2)}) collective-permute-start(bf16[16,2176]{1,0:T(8,128)(2,1)S(1)} %pad_maximum_fusion.4), channel_id=1, source_target_pairs={{0,4},{1,5},{2,6},{3,7},{4,0},{5,1},{6,2},{7,3},{8,12},{9,13},{10,... | collective-permute-start | bytes 208904 | tf_op jit(solution)/shard_map/ppermute | solution.py:143
  10.2 0.8 %collective-permute-done = bf16[8,2048]{1,0:T(8,128)(2,1)S(1)} collective-permute-done((bf16[8,2048]{1,0:T(8,128)(2,1)S(1)}, bf16[8,2048]{1,0:T(8,128)(2,1)S(1)}, u32[]{:S(2)}, u32[]{:S(2)}) %collective-permute-start) | collective-permute-done | bytes 32800 | tf_op jit(solution)/shard_map/ppermute | solution.py:143
  11.0 1.5 %collective-permute-start.2 = (bf16[16,2048]{1,0:T(8,128)(2,1)S(1)}, bf16[16,2048]{1,0:T(8,128)(2,1)S(1)}, u32[]{:S(2)}, u32[]{:S(2)}) collective-permute-start(bf16[16,2048]{1,0:T(8,128)(2,1)S(1)} %pad_maximum_fusion.5), channel_id=1, source_target_pairs={{0,2},{1,3},{2,0},{3,1},{4,6},{5,7},{6,4},{7,5},{8,10},{9,11},{10,... | collective-permute-start | bytes 196616 | tf_op jit(solution)/shard_map/ppermute | solution.py:143
  12.5 0.3 collective-permute-done.3
  12.8 1.8 %collective-permute-start.5 = (bf16[32,2176]{1,0:T(8,128)(2,1)S(1)}, bf16[32,2176]{1,0:T(8,128)(2,1)S(1)}, u32[]{:S(2)}, u32[]{:S(2)}) collective-permute-start(bf16[32,2176]{1,0:T(8,128)(2,1)S(1)} %pad_maximum_fusion.2), channel_id=1, source_target_pairs={{0,2},{1,3},{2,0},{3,1},{4,6},{5,7},{6,4},{7,5},{8,10},{9,11},{10,... | collective-permute-start | bytes 417800 | tf_op jit(solution)/shard_map/ppermute | solution.py:143
  14.6 1.1 %collective-permute-done.2 = bf16[16,2048]{1,0:T(8,128)(2,1)S(1)} collective-permute-done((bf16[16,2048]{1,0:T(8,128)(2,1)S(1)}, bf16[16,2048]{1,0:T(8,128)(2,1)S(1)}, u32[]{:S(2)}, u32[]{:S(2)}) %collective-permute-start.2) | collective-permute-done | bytes 65568 | tf_op jit(solution)/shard_map/ppermute | solution.py:143
  15.8 1.5 %collective-permute-start.4 = (bf16[32,2048]{1,0:T(8,128)(2,1)S(1)}, bf16[32,2048]{1,0:T(8,128)(2,1)S(1)}, u32[]{:S(2)}, u32[]{:S(2)}) collective-permute-start(bf16[32,2048]{1,0:T(8,128)(2,1)S(1)} %pad_maximum_fusion.3), channel_id=1, source_target_pairs={{0,4},{1,5},{2,6},{3,7},{4,0},{5,1},{6,2},{7,3},{8,12},{9,13},{10,... | collective-permute-start | bytes 393224 | tf_op jit(solution)/shard_map/ppermute | solution.py:143
  17.2 0.7 %collective-permute-done.5 = bf16[32,2176]{1,0:T(8,128)(2,1)S(1)} collective-permute-done((bf16[32,2176]{1,0:T(8,128)(2,1)S(1)}, bf16[32,2176]{1,0:T(8,128)(2,1)S(1)}, u32[]{:S(2)}, u32[]{:S(2)}) %collective-permute-start.5) | collective-permute-done | bytes 139296 | tf_op jit(solution)/shard_map/ppermute | solution.py:143
  18.0 0.1 collective-permute-start.7
  18.0 2.8 %collective-permute-done.4 = bf16[32,2048]{1,0:T(8,128)(2,1)S(1)} collective-permute-done((bf16[32,2048]{1,0:T(8,128)(2,1)S(1)}, bf16[32,2048]{1,0:T(8,128)(2,1)S(1)}, u32[]{:S(2)}, u32[]{:S(2)}) %collective-permute-start.4) | collective-permute-done | bytes 131104 | tf_op jit(solution)/shard_map/ppermute | solution.py:143
  20.8 0.0 copy-start
  20.8 0.0 copy-start.1
  20.8 0.1 collective-permute-start.6
  20.9 0.0 collective-permute-done.7.refs_3_.refs_5_.refs_7_
  20.9 5.9 %shard_map.84 = (bf16[512,2048]{1,0:T(8,128)(2,1)}, bf16[512,2048]{1,0:T(8,128)(2,1)}, f32[64,2048]{1,0:T(8,128)S(1)}, f32[64,2048]{1,0:T(8,128)S(1)}) custom-call(bf16[512,2048]{1,0:T(8,128)(2,1)} %refs_0_.3, bf16[512,2048]{1,0:T(8,128)(2,1)} %refs_1_.3, bf16[64,2176]{1,0:T(8,128)(2,1)S(1)} %pad_maximum_fusion.refs_2_.refs_4_.refs_6_, ...), custom_call_target="tpu_custom_call" | custom-call | flops 1610612736 | bytes 6291456 | tf_op jit(solution)/shard_map/pallas_call | solution.py:99
  26.8 0.3 collective-permute-start.8
  27.1 0.0 collective-permute-done.6.refs_3_.refs_5_
  27.1 0.0 copy-done
  27.1 0.0 copy-done.1
  27.1 4.8 %shard_map.85 = (bf16[512,2048]{1,0:T(8,128)(2,1)}, bf16[512,2048]{1,0:T(8,128)(2,1)}, f32[64,2048]{1,0:T(8,128)S(1)}, f32[64,2048]{1,0:T(8,128)S(1)}) custom-call(bf16[512,2048]{1,0:T(8,128)(2,1)S(1)} %copy-done, bf16[512,2048]{1,0:T(8,128)(2,1)S(1)} %copy-done.1, ...), custom_call_target="tpu_custom_call", output_to_operand_aliasing={{0}: (8, {}), {1}: (9, {})} | custom-call | flops 1610612736 | bytes 6291456 | tf_op jit(solution)/shard_map/pallas_call | solution.py:99
  32.0 0.2 collective-permute-start.12
  32.2 0.0 collective-permute-done.8
  32.2 0.1 add.24
  32.2 1.1 %collective-permute-start.9 = (f32[32,2048]{1,0:T(8,128)S(1)}, f32[32,2048]{1,0:T(8,128)S(1)}, u32[]{:S(2)}, u32[]{:S(2)}) collective-permute-start(f32[32,2048]{1,0:T(8,128)S(1)} %slice.75), channel_id=1, source_target_pairs={{0,2},{1,3},{2,0},{3,1},{4,6},{5,7},{6,4},{7,5},{8,10},{9,11},{10,... | collective-permute-start | bytes 786440 | tf_op jit(solution)/shard_map/ppermute | solution.py:143
  33.4 0.5 collective-permute-done.12
  33.9 0.1 add.28
  34.0 1.5 %collective-permute-start.13 = (f32[32,2048]{1,0:T(8,128)S(1)}, f32[32,2048]{1,0:T(8,128)S(1)}, u32[]{:S(2)}, u32[]{:S(2)}) collective-permute-start(f32[32,2048]{1,0:T(8,128)S(1)} %slice.81), channel_id=1, source_target_pairs={{0,4},{1,5},{2,6},{3,7},{4,0},{5,1},{6,2},{7,3},{8,12},{9,13},{10,... | collective-permute-start | bytes 786440 | tf_op jit(solution)/shard_map/ppermute | solution.py:143
  35.4 5.4 %collective-permute-done.9 = f32[32,2048]{1,0:T(8,128)S(1)} collective-permute-done((f32[32,2048]{1,0:T(8,128)S(1)}, f32[32,2048]{1,0:T(8,128)S(1)}, u32[]{:S(2)}, u32[]{:S(2)}) %collective-permute-start.9) | collective-permute-done | bytes 262176 | tf_op jit(solution)/shard_map/ppermute | solution.py:143
  40.9 1.5 %collective-permute-start.10 = (f32[16,2048]{1,0:T(8,128)S(1)}, f32[16,2048]{1,0:T(8,128)S(1)}, u32[]{:S(2)}, u32[]{:S(2)}) collective-permute-start(f32[16,2048]{1,0:T(8,128)S(1)} %slice.77), channel_id=1, source_target_pairs={{0,4},{1,5},{2,6},{3,7},{4,0},{5,1},{6,2},{7,3},{8,12},{9,13},{10,... | collective-permute-start | bytes 393224 | tf_op jit(solution)/shard_map/ppermute | solution.py:143
  42.4 0.1 collective-permute-done.13
  42.5 1.5 %collective-permute-start.14 = (f32[16,2048]{1,0:T(8,128)S(1)}, f32[16,2048]{1,0:T(8,128)S(1)}, u32[]{:S(2)}, u32[]{:S(2)}) collective-permute-start(f32[16,2048]{1,0:T(8,128)S(1)} %slice.83), channel_id=1, source_target_pairs={{0,2},{1,3},{2,0},{3,1},{4,6},{5,7},{6,4},{7,5},{8,10},{9,11},{10,... | collective-permute-start | bytes 393224 | tf_op jit(solution)/shard_map/ppermute | solution.py:143
  44.0 1.9 %collective-permute-done.10 = f32[16,2048]{1,0:T(8,128)S(1)} collective-permute-done((f32[16,2048]{1,0:T(8,128)S(1)}, f32[16,2048]{1,0:T(8,128)S(1)}, u32[]{:S(2)}, u32[]{:S(2)}) %collective-permute-start.10) | collective-permute-done | bytes 131104 | tf_op jit(solution)/shard_map/ppermute | solution.py:143
  46.0 2.5 %collective-permute-start.11 = (f32[8,2048]{1,0:T(8,128)S(1)}, f32[8,2048]{1,0:T(8,128)S(1)}, u32[]{:S(2)}, u32[]{:S(2)}) collective-permute-start(f32[8,2048]{1,0:T(8,128)S(1)} %slice.79), channel_id=1, source_target_pairs={{0,8},{1,9},{2,10},{3,11},{4,12},{5,13},{6,14},{7,15},{8,0},{9,1},... | collective-permute-start | bytes 196616 | tf_op jit(solution)/shard_map/ppermute | solution.py:143
  48.5 0.0 collective-permute-done.14
  48.5 1.6 %collective-permute-start.15 = (f32[8,2048]{1,0:T(8,128)S(1)}, f32[8,2048]{1,0:T(8,128)S(1)}, u32[]{:S(2)}, u32[]{:S(2)}) collective-permute-start(f32[8,2048]{1,0:T(8,128)S(1)} %slice.85), channel_id=1, source_target_pairs={{0,8},{1,9},{2,10},{3,11},{4,12},{5,13},{6,14},{7,15},{8,0},{9,1},... | collective-permute-start | bytes 196616 | tf_op jit(solution)/shard_map/ppermute | solution.py:143
  50.1 2.9 %collective-permute-done.11 = f32[8,2048]{1,0:T(8,128)S(1)} collective-permute-done((f32[8,2048]{1,0:T(8,128)S(1)}, f32[8,2048]{1,0:T(8,128)S(1)}, u32[]{:S(2)}, u32[]{:S(2)}) %collective-permute-start.11) | collective-permute-done | bytes 65568 | tf_op jit(solution)/shard_map/ppermute | solution.py:143
  53.0 0.8 %collective-permute-done.15 = f32[8,2048]{1,0:T(8,128)S(1)} collective-permute-done((f32[8,2048]{1,0:T(8,128)S(1)}, f32[8,2048]{1,0:T(8,128)S(1)}, u32[]{:S(2)}, u32[]{:S(2)}) %collective-permute-start.15) | collective-permute-done | bytes 65568 | tf_op jit(solution)/shard_map/ppermute | solution.py:143
  53.8 0.6 %slice_bitcast_fusion = (bf16[8,2048]{1,0:T(8,128)(2,1)}, bf16[8,2048]{1,0:T(8,128)(2,1)}) fusion(bf16[8,16,2,128]{3,0,2,1:T(8,128)(2,1)S(1)} %bitcast.7), kind=kLoop, calls=%fused_computation.14 | loop fusion | bytes 131072 | tf_op jit(solution)/shard_map/convert_element_type | solution.py:189
  (22 shorter events, 0.3 us)
Async XLA Ops:
  2.1 6.3 %collective-permute-start.1 = (bf16[8,2176]{1,0:T(8,128)(2,1)S(1)}, bf16[8,2176]{1,0:T(8,128)(2,1)S(1)}, u32[]{:S(2)}, u32[]{:S(2)}) collective-permute-start(bf16[8,2176]{1,0:T(8,128)(2,1)S(1)} %pad_maximum_fusion.6), channel_id=1, source_target_pairs={{0,8},{1,9},{2,10},{3,11},{4,12},{5,13},{6,14},{7,15},{8,0},{9,1},... | collective-permute-start | bytes 104456 | tf_op jit(solution)/shard_map/ppermute | solution.py:143
  6.2 4.8 %collective-permute-start = (bf16[8,2048]{1,0:T(8,128)(2,1)S(1)}, bf16[8,2048]{1,0:T(8,128)(2,1)S(1)}, u32[]{:S(2)}, u32[]{:S(2)}) collective-permute-start(bf16[8,2048]{1,0:T(8,128)(2,1)S(1)} %pad_maximum_fusion.7), channel_id=1, source_target_pairs={{0,8},{1,9},{2,10},{3,11},{4,12},{5,13},{6,14},{7,15},{8,0},{9,1},... | collective-permute-start | bytes 98312 | tf_op jit(solution)/shard_map/ppermute | solution.py:143
  8.5 4.3 %collective-permute-start.3 = (bf16[16,2176]{1,0:T(8,128)(2,1)S(1)}, bf16[16,2176]{1,0:T(8,128)(2,1)S(1)}, u32[]{:S(2)}, u32[]{:S(2)}) collective-permute-start(bf16[16,2176]{1,0:T(8,128)(2,1)S(1)} %pad_maximum_fusion.4), channel_id=1, source_target_pairs={{0,4},{1,5},{2,6},{3,7},{4,0},{5,1},{6,2},{7,3},{8,12},{9,13},{10,... | collective-permute-start | bytes 208904 | tf_op jit(solution)/shard_map/ppermute | solution.py:143
  11.0 4.7 %collective-permute-start.2 = (bf16[16,2048]{1,0:T(8,128)(2,1)S(1)}, bf16[16,2048]{1,0:T(8,128)(2,1)S(1)}, u32[]{:S(2)}, u32[]{:S(2)}) collective-permute-start(bf16[16,2048]{1,0:T(8,128)(2,1)S(1)} %pad_maximum_fusion.5), channel_id=1, source_target_pairs={{0,2},{1,3},{2,0},{3,1},{4,6},{5,7},{6,4},{7,5},{8,10},{9,11},{10,... | collective-permute-start | bytes 196616 | tf_op jit(solution)/shard_map/ppermute | solution.py:143
  12.8 5.1 %collective-permute-start.5 = (bf16[32,2176]{1,0:T(8,128)(2,1)S(1)}, bf16[32,2176]{1,0:T(8,128)(2,1)S(1)}, u32[]{:S(2)}, u32[]{:S(2)}) collective-permute-start(bf16[32,2176]{1,0:T(8,128)(2,1)S(1)} %pad_maximum_fusion.2), channel_id=1, source_target_pairs={{0,2},{1,3},{2,0},{3,1},{4,6},{5,7},{6,4},{7,5},{8,10},{9,11},{10,... | collective-permute-start | bytes 417800 | tf_op jit(solution)/shard_map/ppermute | solution.py:143
  15.8 5.0 %collective-permute-start.4 = (bf16[32,2048]{1,0:T(8,128)(2,1)S(1)}, bf16[32,2048]{1,0:T(8,128)(2,1)S(1)}, u32[]{:S(2)}, u32[]{:S(2)}) collective-permute-start(bf16[32,2048]{1,0:T(8,128)(2,1)S(1)} %pad_maximum_fusion.3), channel_id=1, source_target_pairs={{0,4},{1,5},{2,6},{3,7},{4,0},{5,1},{6,2},{7,3},{8,12},{9,13},{10,... | collective-permute-start | bytes 393224 | tf_op jit(solution)/shard_map/ppermute | solution.py:143
  18.0 3.0 %collective-permute-start.7 = (bf16[64,2176]{1,0:T(8,128)(2,1)S(1)}, bf16[64,2176]{1,0:T(8,128)(2,1)S(1)}, u32[]{:S(2)}, u32[]{:S(2)}) collective-permute-start(bf16[64,2176]{1,0:T(8,128)(2,1)S(1)} %pad_maximum_fusion.refs_2_.refs_4_.refs_6_), channel_id=1, source_target_pairs={{0,1},{1,0},{2,3},{3,2},{4,5},{5,4},{6,7},{7,6},{8,9},{9,8},{10,11... | collective-permute-start | bytes 835592 | tf_op jit(solution)/shard_map/ppermute | solution.py:143
  20.8 6.3 %copy-start = (bf16[512,2048]{1,0:T(8,128)(2,1)S(1)}, bf16[512,2048]{1,0:T(8,128)(2,1)}, u32[]{:S(2)}) copy-start(bf16[512,2048]{1,0:T(8,128)(2,1)} %refs_0_.3) | copy-start | bytes 6291460
  20.8 6.3 %copy-start.1 = (bf16[512,2048]{1,0:T(8,128)(2,1)S(1)}, bf16[512,2048]{1,0:T(8,128)(2,1)}, u32[]{:S(2)}) copy-start(bf16[512,2048]{1,0:T(8,128)(2,1)} %refs_1_.3) | copy-start | bytes 6291460
  20.8 6.3 %collective-permute-start.6 = (bf16[64,2048]{1,0:T(8,128)(2,1)S(1)}, bf16[64,2048]{1,0:T(8,128)(2,1)S(1)}, u32[]{:S(2)}, u32[]{:S(2)}) collective-permute-start(bf16[64,2048]{1,0:T(8,128)(2,1)S(1)} %pad_maximum_fusion.1.refs_2_.refs_4_), channel_id=1, source_target_pairs={{0,1},{1,0},{2,3},{3,2},{4,5},{5,4},{6,7},{7,6},{8,9},{9,8},{10,11... | collective-permute-start | bytes 786440 | tf_op jit(solution)/shard_map/ppermute | solution.py:143
  26.8 5.3 %collective-permute-start.8 = (f32[64,2048]{1,0:T(8,128)S(1)}, f32[64,2048]{1,0:T(8,128)S(1)}, u32[]{:S(2)}, u32[]{:S(2)}) collective-permute-start(f32[64,2048]{1,0:T(8,128)S(1)} %get-tuple-element.23), channel_id=1, source_target_pairs={{0,1},{1,0},{2,3},{3,2},{4,5},{5,4},{6,7},{7,6},{8,9},{9,8},{10,11... | collective-permute-start | bytes 1572872 | tf_op jit(solution)/shard_map/ppermute | solution.py:143
  32.0 1.9 %collective-permute-start.12 = (f32[64,2048]{1,0:T(8,128)S(1)}, f32[64,2048]{1,0:T(8,128)S(1)}, u32[]{:S(2)}, u32[]{:S(2)}) collective-permute-start(f32[64,2048]{1,0:T(8,128)S(1)} %get-tuple-element.25), channel_id=1, source_target_pairs={{0,1},{1,0},{2,3},{3,2},{4,5},{5,4},{6,7},{7,6},{8,9},{9,8},{10,11... | collective-permute-start | bytes 1572872 | tf_op jit(solution)/shard_map/ppermute | solution.py:143
  32.2 8.6 %collective-permute-start.9 = (f32[32,2048]{1,0:T(8,128)S(1)}, f32[32,2048]{1,0:T(8,128)S(1)}, u32[]{:S(2)}, u32[]{:S(2)}) collective-permute-start(f32[32,2048]{1,0:T(8,128)S(1)} %slice.75), channel_id=1, source_target_pairs={{0,2},{1,3},{2,0},{3,1},{4,6},{5,7},{6,4},{7,5},{8,10},{9,11},{10,... | collective-permute-start | bytes 786440 | tf_op jit(solution)/shard_map/ppermute | solution.py:143
  34.0 8.5 %collective-permute-start.13 = (f32[32,2048]{1,0:T(8,128)S(1)}, f32[32,2048]{1,0:T(8,128)S(1)}, u32[]{:S(2)}, u32[]{:S(2)}) collective-permute-start(f32[32,2048]{1,0:T(8,128)S(1)} %slice.81), channel_id=1, source_target_pairs={{0,4},{1,5},{2,6},{3,7},{4,0},{5,1},{6,2},{7,3},{8,12},{9,13},{10,... | collective-permute-start | bytes 786440 | tf_op jit(solution)/shard_map/ppermute | solution.py:143
  40.9 5.0 %collective-permute-start.10 = (f32[16,2048]{1,0:T(8,128)S(1)}, f32[16,2048]{1,0:T(8,128)S(1)}, u32[]{:S(2)}, u32[]{:S(2)}) collective-permute-start(f32[16,2048]{1,0:T(8,128)S(1)} %slice.77), channel_id=1, source_target_pairs={{0,4},{1,5},{2,6},{3,7},{4,0},{5,1},{6,2},{7,3},{8,12},{9,13},{10,... | collective-permute-start | bytes 393224 | tf_op jit(solution)/shard_map/ppermute | solution.py:143
  42.5 6.0 %collective-permute-start.14 = (f32[16,2048]{1,0:T(8,128)S(1)}, f32[16,2048]{1,0:T(8,128)S(1)}, u32[]{:S(2)}, u32[]{:S(2)}) collective-permute-start(f32[16,2048]{1,0:T(8,128)S(1)} %slice.83), channel_id=1, source_target_pairs={{0,2},{1,3},{2,0},{3,1},{4,6},{5,7},{6,4},{7,5},{8,10},{9,11},{10,... | collective-permute-start | bytes 393224 | tf_op jit(solution)/shard_map/ppermute | solution.py:143
  46.0 7.0 %collective-permute-start.11 = (f32[8,2048]{1,0:T(8,128)S(1)}, f32[8,2048]{1,0:T(8,128)S(1)}, u32[]{:S(2)}, u32[]{:S(2)}) collective-permute-start(f32[8,2048]{1,0:T(8,128)S(1)} %slice.79), channel_id=1, source_target_pairs={{0,8},{1,9},{2,10},{3,11},{4,12},{5,13},{6,14},{7,15},{8,0},{9,1},... | collective-permute-start | bytes 196616 | tf_op jit(solution)/shard_map/ppermute | solution.py:143
  48.5 5.2 %collective-permute-start.15 = (f32[8,2048]{1,0:T(8,128)S(1)}, f32[8,2048]{1,0:T(8,128)S(1)}, u32[]{:S(2)}, u32[]{:S(2)}) collective-permute-start(f32[8,2048]{1,0:T(8,128)S(1)} %slice.85), channel_id=1, source_target_pairs={{0,8},{1,9},{2,10},{3,11},{4,12},{5,13},{6,14},{7,15},{8,0},{9,1},... | collective-permute-start | bytes 196616 | tf_op jit(solution)/shard_map/ppermute | solution.py:143
